TPU v7x, 128 devices: a whole 4x4x4 slice. The times are simulated.
128 devices in a mesh: fluid: 32 (over z, y, core), shell: 4 (over x).
Axes of the slice: x: 4, y: 4, z: 4, core: 2. Of those that a mesh axis runs over, the one named last changes fastest.
Arguments:
- traction_base: float32 [32768, 3, 128], P(('fluid', 'shell')), may hold values from -6 to 6
- added_mass: float32 [32768, 128], P(('fluid', 'shell')), may hold values from 0.3 to 3
- interface_prev: float32 [32768, 3, 128], P(('fluid', 'shell')), may hold values from -6 to 6
- patch_route: int32 [32768, 1], P(('fluid', 'shell')), may hold values from 0 to 127; in each aligned block of 256 rows (0 to 255, 256 to 511, ...) at most 4 rows name the same one
- basis_pattern: int32 [32768], P(('fluid', 'shell')), may hold values from 0 to 7
- column_block: int32 [32768], P(('fluid', 'shell')), may hold values from 0 to 3
- basis_values_table: float32 [8, 128, 128], replicated, may hold values from -0.0625 to 0.0625
- stiffness: float32 [1024, 384, 384], P(('fluid', 'shell')), may hold values from -0.21875 to 0.21875
- stiff_row: int32 [1024], P(('fluid', 'shell')), may hold values from 0 to 15
- stiff_col: int32 [1024], P(('fluid', 'shell')), may hold values from 0 to 3
- block_inverse: float32 [512, 384, 384], P(('fluid', 'shell')), may hold values from -1 to 2.5
- previous_shell_displacement: float32 [512, 3, 128], P(('fluid', 'shell')), may hold values from -6 to 6
Outputs:
- shell_disp: float32 [512, 3, 128], P(('fluid', 'shell'))
- interface_disp: float32 [32768, 3, 128], P(('fluid', 'shell'))
Inputs may be any that keep to these rules, and one draw needn't show every extreme that they name: `patch_route`: patch p belongs to index p of fluid+shell. At most 4 of the blocks of one device lie on one patch.
All inputs are finite; a program needn't handle non-finite values.
Results may differ from a plain program's by a relative error of at most 0.0001.
Values sent between devices are 32-bit elements; how exact they have to be, the bound alone decides.
A program may use at most 64 MiB of HBM per device.

v0:
```python
import jax
import jax.numpy as jnp
from jax import lax
from jax.sharding import PartitionSpec as P

ITERS = 2


def couple_rows(displacement_field, stiffness, stiff_col, stiff_hits):
    flat_values = displacement_field.reshape(displacement_field.shape[0], -1)
    products = jnp.einsum(
        "bij,bj->bi", stiffness, flat_values[stiff_col], precision=lax.Precision.HIGHEST
    )
    partial_value = jnp.einsum("bg,bi->gi", stiff_hits, products, precision=lax.Precision.HIGHEST)
    return lax.psum_scatter(partial_value, "shell", scatter_dimension=0, tiled=True)


def on_device(
    traction_base,
    added_mass,
    interface_prev,
    patch_route,
    basis_pattern,
    column_block,
    basis_values_table,
    stiffness,
    stiff_row,
    stiff_col,
    block_inverse,
    previous_shell_displacement,
):
    highest = lax.Precision.HIGHEST
    devices = lax.axis_size(("fluid", "shell"))
    shells = lax.axis_size("shell")
    num_blocks = traction_base.shape[0]
    points = traction_base.shape[2]
    patterns = basis_values_table.shape[0]
    col_count = previous_shell_displacement.shape[0]
    ctrl_points = previous_shell_displacement.shape[2]
    capacity = 2 * num_blocks // devices
    targets = patch_route[:, 0]
    stiff_hits = (
        stiff_row[:, None] == jnp.arange(shells * col_count, dtype=jnp.int32)[None, :]
    ).astype(jnp.float32)
    hits = (targets[:, None] == jnp.arange(devices, dtype=jnp.int32)[None, :]).astype(jnp.int32)
    before = jnp.cumsum(hits, axis=0) - hits
    slot_index = targets * capacity + jnp.sum(before * hits, axis=1)
    sent_pattern = jnp.full((devices * capacity,), -1, jnp.int32).at[slot_index].set(basis_pattern)
    sent_column = jnp.zeros((devices * capacity,), jnp.int32).at[slot_index].set(column_block)
    displacement_field = previous_shell_displacement
    interface = interface_prev
    for iteration in range(ITERS):
        traction = traction_base - added_mass[:, None, :] * interface
        outgoing = (
            jnp.zeros((devices * capacity, 3, points), jnp.float32).at[slot_index].set(traction)
        )
        arrived = lax.all_to_all(
            outgoing, ("fluid", "shell"), split_axis=0, concat_axis=0, tiled=True
        )
        got_pattern = lax.all_to_all(
            sent_pattern, ("fluid", "shell"), split_axis=0, concat_axis=0, tiled=True
        )
        got_column = lax.all_to_all(
            sent_column, ("fluid", "shell"), split_axis=0, concat_axis=0, tiled=True
        )
        gather_codes = jnp.where(got_pattern >= 0, got_column * patterns + got_pattern, -1)
        selector = (
            gather_codes[:, None] == jnp.arange(col_count * patterns, dtype=jnp.int32)[None, :]
        ).astype(jnp.float32)
        grouped = jnp.einsum(
            "rg,rx->gx",
            selector,
            arrived.reshape(devices * capacity, 3 * points),
            precision=highest,
        )
        grouped = grouped.reshape(col_count, patterns, 3, points)
        shell_load_vector = jnp.einsum(
            "knaq,nqc->kac", grouped, basis_values_table, precision=highest
        )
        shell_load_vector, codes = (shell_load_vector, gather_codes)
        coupled_result = couple_rows(displacement_field, stiffness, stiff_col, stiff_hits)
        flat_values = displacement_field.reshape(col_count, 3 * ctrl_points)
        residual_row_values = shell_load_vector.reshape(col_count, 3 * ctrl_points) - coupled_result
        flat_values = flat_values + jnp.einsum(
            "kij,kj->ki", block_inverse, residual_row_values, precision=highest
        )
        displacement_field = flat_values.reshape(col_count, 3, ctrl_points)
        evaluated = jnp.einsum(
            "kac,nqc->knaq", displacement_field, basis_values_table, precision=highest
        )
        evaluated = evaluated.reshape(col_count * patterns, 3, points)
        replies = evaluated[jnp.maximum(codes, 0)]
        returned = lax.all_to_all(
            replies, ("fluid", "shell"), split_axis=0, concat_axis=0, tiled=True
        )
        interface = returned[slot_index]
    return (displacement_field, interface)


def solution(mesh):
    return jax.shard_map(
        on_device,
        mesh=mesh,
        in_specs=(
            P(("fluid", "shell"), None, None),
            P(("fluid", "shell"), None),
            P(("fluid", "shell"), None, None),
            P(("fluid", "shell"), None),
            P(("fluid", "shell")),
            P(("fluid", "shell")),
            P(),
            P(("fluid", "shell"), None, None),
            P(("fluid", "shell")),
            P(("fluid", "shell")),
            P(("fluid", "shell"), None, None),
            P(("fluid", "shell"), None, None),
        ),
        out_specs=(P(("fluid", "shell"), None, None), P(("fluid", "shell"), None, None)),
        check_vma=False,
    )
```

profile of v0, /device:TPU:1, one launch (start us, length us, event | category | flops | bytes accessed | tf_op | source)
XLA Modules:
  0.0 232.8 jit_solution(1074430183814630794)
XLA Ops:
  0.6 0.0 copy-start
  0.6 0.9 copy.55
  1.6 0.2 fusion.13
  1.9 0.9 fusion.15
  2.7 0.7 compare_select_fusion.1
  3.4 1.6 scatter_custom_fusion
  5.0 0.7 all_to_all.26
  5.7 11.5 %all-to-all-start = ((s32[128,4,1]{1,2,0:T(1,128)}), s32[128,4,1]{1,2,0:T(1,128)S(1)}, u32[]{:S(2)}, u32[]{:S(2)}) async-start(s32[128,4,1]{1,2,0:T(1,128)} %bitcast.8), calls=%async_computation | async-start | bytes 131072 | tf_op jit(solution)/shard_map/all_to_all | solution.py:60
  17.2 1.2 multiply_subtract_fusion
  18.4 0.7 compare_select_fusion.2
  19.1 1.6 scatter_custom_fusion.1
  20.6 0.7 all_to_all.28
  21.4 5.5 %all-to-all-done = s32[128,4,1]{1,2,0:T(1,128)S(1)} async-done(((s32[128,4,1]{1,2,0:T(1,128)}), s32[128,4,1]{1,2,0:T(1,128)S(1)}, u32[]{:S(2)}, u32[]{:S(2)}) %all-to-all-start) | async-done | bytes 2080 | tf_op jit(solution)/shard_map/all_to_all | solution.py:60
  26.9 4.3 %all-to-all-start.1 = ((s32[128,4,1]{1,2,0:T(1,128)}), s32[128,4,1]{1,2,0:T(1,128)S(1)}, u32[]{:S(2)}, u32[]{:S(2)}) async-start(s32[128,4,1]{1,2,0:T(1,128)} %bitcast.9), calls=%async_computation.1 | async-start | bytes 131072 | tf_op jit(solution)/shard_map/all_to_all | solution.py:63
  31.1 0.3 copy.59
  31.4 1.3 gather_fusion
  32.7 0.0 copy-start.4
  32.7 0.0 copy-start.3
  32.7 1.2 broadcast.125.clone
  33.9 24.4 %scatter_fusion = f32[512,3,128]{2,1,0:T(4,128)} fusion(f32[512,3,128]{2,1,0:T(4,128)} %broadcast.125.clone, s32[256]{0:T(256)S(1)} %bitcast.143, f32[256,3,128]{2,1,0:T(4,128)S(1)} %copy.59), kind=kCustom, calls=%fused_computation.8 | custom fusion | bytes 1180672 | tf_op jit(solution)/shard_map/scatter | solution.py:55
  58.3 0.0 all-to-all-done.1
  58.3 10.2 %all-to-all-start.2 = ((f32[512,3,128]{2,1,0:T(4,128)}), f32[512,3,128]{2,1,0:T(4,128)}, u32[]{:S(2)}, u32[]{:S(2)}) async-start(f32[512,3,128]{2,1,0:T(4,128)} %scatter_fusion), calls=%async_computation.2 | async-start | bytes 2097152 | tf_op jit(solution)/shard_map/all_to_all | solution.py:57
  68.5 0.0 copy-start.2
  68.5 6.6 %fusion.34 = f32[8,1,384]{2,1,0:T(1,128)S(1)} fusion(f32[8,384,384]{2,1,0:T(8,128)} %param.19, f32[8,384,1]{1,0,2:T(8,128)S(1)} %bitcast.138), kind=kOutput, calls=%fused_computation.58 | convolution fusion | flops 14155776 | bytes 4743168 | tf_op jit(solution)/shard_map/bij,bj->bi/dot_general | solution.py:11
  75.1 0.0 copy-done.4
  75.1 0.6 dynamic-slice
  76.4 0.0 copy-done.3
  76.4 0.3 fusion.28
  76.6 14.2 %all-reduce = f32[16,384]{1,0:T(8,128)S(1)} all-reduce(f32[16,384]{1,0:T(8,128)S(1)} %fusion.28), channel_id=2, replica_groups=mesh['fluid'=32,'shell'=4] {'shell'}, use_global_device_ids=true, to_apply=%region_6.7.clone | all-reduce | flops 6144 | bytes 49152
  90.8 0.5 broadcast.163
  91.3 1.1 maximum_reduce_fusion
  92.4 0.1 reshape.157
  92.5 0.1 select_n.36
  92.6 0.0 all-to-all-done.2
  92.6 2.4 %copy.60 = f32[512,3,128]{0,2,1:T(8,128)} copy(f32[512,3,128]{2,1,0:T(4,128)} %all-to-all-done.2) | data formatting | bytes 1572864 | tf_op jit(solution)/shard_map/all_to_all | solution.py:57
  95.1 1.7 fusion.6
  96.8 0.4 fusion.3
  97.2 2.2 fusion.40
  99.4 0.5 convolution_bitcast_fusion.1
  100.0 2.6 %gather_fusion.1 = f32[512,3,128]{2,1,0:T(4,128)} fusion(f32[32,3,128]{2,1,0:T(4,128)S(1)} %copy.62, s32[1024]{0:T(1024)S(1)} %pad_clamp_fusion.1), kind=kCustom, calls=%fused_computation.1 | custom fusion | bytes 1574912 | tf_op jit(solution)/shard_map/gather | solution.py:92
  102.6 11.5 %all-to-all-start.3 = ((f32[512,3,128]{2,1,0:T(4,128)}), f32[512,3,128]{2,1,0:T(4,128)}, u32[]{:S(2)}, u32[]{:S(2)}) async-start(f32[512,3,128]{2,1,0:T(4,128)} %gather_fusion.1), calls=%async_computation.3 | async-start | bytes 2097152 | tf_op jit(solution)/shard_map/all_to_all | solution.py:93
  114.2 19.2 %all-to-all-done.3 = f32[512,3,128]{2,1,0:T(4,128)} async-done(((f32[512,3,128]{2,1,0:T(4,128)}), f32[512,3,128]{2,1,0:T(4,128)}, u32[]{:S(2)}, u32[]{:S(2)}) %all-to-all-start.3) | async-done | bytes 786464 | tf_op jit(solution)/shard_map/all_to_all | solution.py:93
  133.3 2.2 gather_fusion.2
  135.6 1.1 fusion.12
  136.7 0.3 copy.64
  136.9 1.2 broadcast.125
  138.1 24.4 %scatter_fusion.1 = f32[512,3,128]{2,1,0:T(4,128)} fusion(f32[512,3,128]{2,1,0:T(4,128)} %broadcast.125, s32[256]{0:T(256)S(1)} %bitcast.145, f32[256,3,128]{2,1,0:T(4,128)S(1)} %copy.64), kind=kCustom, calls=%fused_computation.9 | custom fusion | bytes 1180672 | tf_op jit(solution)/shard_map/scatter | solution.py:55
  162.5 4.9 %all-to-all-start.4 = ((f32[512,3,128]{2,1,0:T(4,128)}), f32[512,3,128]{2,1,0:T(4,128)}, u32[]{:S(2)}, u32[]{:S(2)}) async-start(f32[512,3,128]{2,1,0:T(4,128)} %scatter_fusion.1), calls=%async_computation.4 | async-start | bytes 2097152 | tf_op jit(solution)/shard_map/all_to_all | solution.py:57
  167.4 0.6 gather_fusion.3
  167.9 6.6 %fusion.31 = f32[8,1,384]{2,1,0:T(1,128)S(1)} fusion(f32[8,384,384]{2,1,0:T(8,128)} %param.19, f32[8,384,1]{1,0,2:T(8,128)S(1)} %bitcast.139), kind=kOutput, calls=%fused_computation.55 | convolution fusion | flops 14155776 | bytes 4743168 | tf_op jit(solution)/shard_map/bij,bj->bi/dot_general | solution.py:11
  174.5 0.3 fusion.26
  174.8 14.2 %all-reduce.1 = f32[16,384]{1,0:T(8,128)S(1)} all-reduce(f32[16,384]{1,0:T(8,128)S(1)} %fusion.26), channel_id=3, replica_groups=mesh['fluid'=32,'shell'=4] {'shell'}, use_global_device_ids=true, to_apply=%region_8.9.clone | all-reduce | flops 6144 | bytes 49152
  189.0 0.0 all-to-all-done.4
  189.0 2.4 %copy.65 = f32[512,3,128]{0,2,1:T(8,128)} copy(f32[512,3,128]{2,1,0:T(4,128)} %all-to-all-done.4) | data formatting | bytes 1572864 | tf_op jit(solution)/shard_map/all_to_all | solution.py:57
  191.4 1.7 fusion.4
  193.1 0.4 fusion.2
  193.5 2.2 fusion.38
  195.7 0.5 convolution_bitcast_fusion
  196.3 2.6 %gather_fusion.4 = f32[512,3,128]{2,1,0:T(4,128)} fusion(f32[32,3,128]{2,1,0:T(4,128)S(1)} %copy.67, s32[1024]{0:T(1024)S(1)} %pad_clamp_fusion.1), kind=kCustom, calls=%fused_computation.4 | custom fusion | bytes 1574912 | tf_op jit(solution)/shard_map/gather | solution.py:92
  199.0 11.6 %all-to-all-start.5 = ((f32[512,3,128]{2,1,0:T(4,128)}), f32[512,3,128]{2,1,0:T(4,128)}, u32[]{:S(2)}, u32[]{:S(2)}) async-start(f32[512,3,128]{2,1,0:T(4,128)} %gather_fusion.4), calls=%async_computation.5 | async-start | bytes 2097152 | tf_op jit(solution)/shard_map/all_to_all | solution.py:93
  210.6 0.6 fusion.44
  211.2 18.6 %all-to-all-done.5 = f32[512,3,128]{2,1,0:T(4,128)} async-done(((f32[512,3,128]{2,1,0:T(4,128)}), f32[512,3,128]{2,1,0:T(4,128)}, u32[]{:S(2)}, u32[]{:S(2)}) %all-to-all-start.5) | async-done | bytes 786464 | tf_op jit(solution)/shard_map/all_to_all | solution.py:93
  229.8 2.2 gather_fusion.5
  232.0 0.8 copy.68
  (19 shorter events, 0.2 us)
Async XLA Ops:
  0.6 96.5 %copy-start = (f32[4,384,384]{2,1,0:T(8,128)S(1)}, f32[4,384,384]{2,1,0:T(8,128)}, u32[]{:S(2)}) copy-start(f32[4,384,384]{2,1,0:T(8,128)} %param.22) | copy-start | bytes 7077892
  5.7 21.1 %all-to-all-start = ((s32[128,4,1]{1,2,0:T(1,128)}), s32[128,4,1]{1,2,0:T(1,128)S(1)}, u32[]{:S(2)}, u32[]{:S(2)}) async-start(s32[128,4,1]{1,2,0:T(1,128)} %bitcast.8), calls=%async_computation | async-start | bytes 131072 | tf_op jit(solution)/shard_map/all_to_all | solution.py:60
  26.9 31.4 %all-to-all-start.1 = ((s32[128,4,1]{1,2,0:T(1,128)}), s32[128,4,1]{1,2,0:T(1,128)S(1)}, u32[]{:S(2)}, u32[]{:S(2)}) async-start(s32[128,4,1]{1,2,0:T(1,128)} %bitcast.9), calls=%async_computation.1 | async-start | bytes 131072 | tf_op jit(solution)/shard_map/all_to_all | solution.py:63
  32.7 42.4 %copy-start.4 = (u32[128]{0:T(128)S(1)}, u32[128]{0:T(128)}, u32[]{:S(2)}) copy-start(u32[128]{0:T(128)} %constant.31) | copy-start | bytes 1540
  32.7 43.7 %copy-start.3 = (s32[8]{0:T(128)S(1)}, s32[8]{0:T(128)}, u32[]{:S(2)}) copy-start(s32[8]{0:T(128)} %param.20) | copy-start | bytes 100
  58.3 38.5 %copy-start.1 = (f32[8,128,128]{2,1,0:T(8,128)S(1)}, f32[8,128,128]{2,1,0:T(8,128)}, u32[]{:S(2)}) copy-start(f32[8,128,128]{2,1,0:T(8,128)} %param.18) | copy-start | bytes 1572868
  58.3 34.4 %all-to-all-start.2 = ((f32[512,3,128]{2,1,0:T(4,128)}), f32[512,3,128]{2,1,0:T(4,128)}, u32[]{:S(2)}, u32[]{:S(2)}) async-start(f32[512,3,128]{2,1,0:T(4,128)} %scatter_fusion), calls=%async_computation.2 | async-start | bytes 2097152 | tf_op jit(solution)/shard_map/all_to_all | solution.py:57
  68.5 30.9 %copy-start.2 = (f32[4,3,128]{2,0,1:T(4,128)S(1)}, f32[4,3,128]{2,0,1:T(4,128)}, u32[]{:S(2)}) copy-start(f32[4,3,128]{2,0,1:T(4,128)} %param.23) | copy-start | bytes 18436
  102.6 30.7 %all-to-all-start.3 = ((f32[512,3,128]{2,1,0:T(4,128)}), f32[512,3,128]{2,1,0:T(4,128)}, u32[]{:S(2)}, u32[]{:S(2)}) async-start(f32[512,3,128]{2,1,0:T(4,128)} %gather_fusion.1), calls=%async_computation.3 | async-start | bytes 2097152 | tf_op jit(solution)/shard_map/all_to_all | solution.py:93
  162.5 26.6 %all-to-all-start.4 = ((f32[512,3,128]{2,1,0:T(4,128)}), f32[512,3,128]{2,1,0:T(4,128)}, u32[]{:S(2)}, u32[]{:S(2)}) async-start(f32[512,3,128]{2,1,0:T(4,128)} %scatter_fusion.1), calls=%async_computation.4 | async-start | bytes 2097152 | tf_op jit(solution)/shard_map/all_to_all | solution.py:57
  199.0 30.8 %all-to-all-start.5 = ((f32[512,3,128]{2,1,0:T(4,128)}), f32[512,3,128]{2,1,0:T(4,128)}, u32[]{:S(2)}, u32[]{:S(2)}) async-start(f32[512,3,128]{2,1,0:T(4,128)} %gather_fusion.4), calls=%async_computation.5 | async-start | bytes 2097152 | tf_op jit(solution)/shard_map/all_to_all | solution.py:93
where the time goes:
time: 235 us; the launch traced here: 233 us
  local copies, waits for them, and re-layouts  75.8 us (32%)
  starting transfers between devices  54 us (23%)
  waiting for transfers between devices  43.2 us (18%)
  blocking collectives  28.4 us (12%)
  matrix products  23.4 us (10%)
  other arithmetic  6.43 us (3%)
    scatter x2, local copies, waits for them, and re-layouts, on_device(): jnp.zeros((devices * capacity, 3, points), jnp.float32).at[slot_index]  48.7 us
    all_to_all x2, waiting for transfers between devices, on_device(): lax.all_to_all(replies, ('fluid', 'shell'), split_axis=0, concat_axis=0,...  37.7 us
    unnamed x2, blocking collectives  28.4 us
    all_to_all x2, starting transfers between devices, on_device(): lax.all_to_all(replies, ('fluid', 'shell'), split_axis=0, concat_axis=0,...  23.1 us
    all_to_all x2, starting transfers between devices, on_device(): lax.all_to_all(outgoing, ('fluid', 'shell'), split_axis=0, concat_axis=0,...  15.1 us
    dot_general x2, matrix products, couple_rows(): jnp.einsum('bij,bj->bi', stiffness, flat_values[stiff_col], precision=lax...  13.2 us
    all_to_all x1, starting transfers between devices, on_device(): lax.all_to_all(sent_pattern, ('fluid', 'shell'), split_axis=0, concat_axi...  11.5 us
    all_to_all x1, waiting for transfers between devices, on_device(): lax.all_to_all(sent_pattern, ('fluid', 'shell'), split_axis=0, concat_axi...  5.51 us
  transfers between devices with their start and end apart: 6, of which 3 were waited for; matrix products, arithmetic and copies ran while one was open for 21% of the time, Pallas kernels for 0%

commit v1 on v0

v1 whole, which is shorter than its diff:
```python
import functools

import jax
import jax.numpy as jnp
from jax import lax
from jax.experimental import pallas as pl
from jax.experimental.pallas import tpu as pltpu
from jax.sharding import PartitionSpec as P

F32, BF16, I32 = jnp.float32, jnp.bfloat16, jnp.int32
NT = (((1,), (1,)), ((), ()))
NN = (((1,), (0,)), ((), ()))
PART_W = ((0, 1, 2), (3, 4, 5), (6, 7))
REST = ((0, 4), (4, 8), (8, 11))
FIRST = ((0, 1), (1, 2), (2, 3))


def split(value):
    high = value.astype(BF16)
    low = (value - high.astype(F32)).astype(BF16)
    return high, low


def dot(a, b, dims=NN):
    return lax.dot_general(a, b, dims, preferred_element_type=F32)


def kernel(
    n,
    base_h,
    mass_h,
    prev_h,
    route_ref,
    pattern_ref,
    column_ref,
    table_h,
    stiff_h,
    srow_ref,
    scol_ref,
    inverse_h,
    start_ref,
    out_u,
    out_i,
    base_v,
    mass_v,
    prev_v,
    table_v,
    stiff_v,
    inverse_v,
    stiff_hi,
    stiff_lo,
    inverse_hi,
    inverse_lo,
    nn_w,
    nt_w,
    nt_lo,
    codes,
    pmask,
    scatter_hot,
    gather_hot,
    d_first,
    d_rest,
    c_first,
    c_rest,
    r1_first,
    r1_rest,
    f_first,
    f_rest,
    r2_first,
    r2_rest,
    g_first,
    g_rest,
    r3_first,
    r3_rest,
    cpl_out,
    cpl_in,
    rows_s,
    wide_s,
    gather3,
    field,
    load_sem,
    core_send,
    core_recv,
    axis_send,
    axis_recv,
    cpl_send,
    cpl_recv,
    back_send,
    back_recv,
    home_send,
    home_recv,
):
    fluid, x = lax.axis_index("fluid"), lax.axis_index("shell")
    core = lax.rem(fluid, 2)
    y = lax.rem(lax.div(fluid, 2), n)
    z = lax.div(fluid, 2 * n)
    cols = 4
    half, rows1, rows2 = n * n * n * cols, n * n * cols, n * cols
    blocks = mass_v.shape[0]
    patterns = table_v.shape[0]
    points = table_v.shape[1]
    keys = 2 * half

    def at(axis, step):
        if axis == 0:
            return (fluid, lax.rem(x + step, n))
        if axis == 1:
            return ((z * n + lax.rem(y + step, n)) * 2 + core, x)
        return ((lax.rem(z + step, n) * n + y) * 2 + core, x)

    sibling = (fluid + 1 - 2 * core, x)
    place = (x, y, z)
    axes = ((0, 1, 2), (1, 2, 0), (2, 0, 1))
    MESH = pl.DeviceIdType.MESH

    loads = [
        pltpu.make_async_copy(src, dst, load_sem.at[i])
        for i, (src, dst) in enumerate(
            (
                (mass_h, mass_v),
                (prev_h, prev_v),
                (base_h, base_v),
                (table_h, table_v),
                (stiff_h, stiff_v),
                (inverse_h, inverse_v),
            )
        )
    ]
    for copy in loads:
        copy.start()

    barrier = pltpu.get_barrier_semaphore()
    partners = [sibling] + [at(axis, step) for axis in range(3) for step in range(1, n)]
    for partner in partners:
        pl.semaphore_signal(barrier, inc=1, device_id=partner, device_id_type=MESH)

    route, column, pattern = route_ref[...], column_ref[...], pattern_ref[...]
    bits = n.bit_length() - 1
    px = route & (n - 1)
    pcore = (route >> bits) & 1
    py = (route >> (bits + 1)) & (n - 1)
    pz = route >> (2 * bits + 1)
    where_is = (px, py, pz)
    code = [
        (((pcore * n + where_is[a]) * n + where_is[b]) * n + where_is[c]) * cols + column
        for a, b, c in axes
    ]
    codes[...] = jnp.zeros_like(codes)
    for part in range(3):
        codes[part : part + 1, :] = code[part].astype(F32)
    codes[3:4, :] = pattern.astype(F32)
    flipped = codes[...].T
    pattern_col = flipped[:, 3:4]
    for p in range(patterns):
        pmask[p] = jnp.broadcast_to(jnp.where(pattern_col == p, 1.0, 0.0), (blocks, points)).astype(BF16)
    sub = lax.broadcasted_iota(I32, (keys, blocks), 0)
    for part in range(3):
        scatter_hot[part] = jnp.where(sub == code[part], 1.0, 0.0).astype(BF16)

    loads[0].wait()
    high, low = split(mass_v[...])
    for part in range(3):
        for j, p in enumerate(PART_W[part]):
            masked = jnp.concatenate([high * pmask[p], low * pmask[p]], axis=1)
            summed = dot(scatter_hot[part], masked)
            d_rest[REST[part][0] + 1 + j] = summed[:, :points] + summed[:, points:]

    loads[3].wait()
    for p in range(patterns):
        th, tl = split(table_v[p])
        spot = slice(p * points, (p + 1) * points)
        nn_w[spot, :points] = th
        nn_w[spot, points:] = tl
        nt_w[spot, :points] = th
        nt_w[spot, points:] = th
        nt_lo[spot, :] = tl

    def project(value):
        vh, vl = split(value)
        both = None
        for v in (vh, vl):
            wide = jnp.concatenate([v * pmask[p] for p in range(patterns)], axis=1)
            got = dot(wide, nn_w[...])
            both = got if both is None else both + got
        ph, pl_ = split(both[:, :points] + both[:, points:])
        return jnp.concatenate([ph, pl_], axis=1)

    loads[1].wait()
    loads[2].wait()
    for part in range(3):
        force = base_v[part] - mass_v[...] * prev_v[part]
        summed = dot(scatter_hot[part], project(force))
        d_first[part] = summed[:, :points] + summed[:, points:]
    pl.semaphore_wait(barrier, len(partners))
    other = (1 - core) * half
    mine = core * half

    def to_sibling(group, source, target):
        return pltpu.make_async_remote_copy(
            src_ref=source.at[:, pl.ds(other, half), :],
            dst_ref=target,
            send_sem=core_send.at[group],
            recv_sem=core_recv.at[group],
            device_id=sibling,
            device_id_type=MESH,
        )

    core_copies = [to_sibling(0, d_first, c_first), to_sibling(1, d_rest, c_rest)]
    core_copies[0].start()
    for part in range(3):
        summed = dot(scatter_hot[part], project(base_v[part]))
        d_rest[REST[part][0]] = summed[:, :points] + summed[:, points:]
    core_copies[1].start()

    loads[4].wait()
    for i in range(stiff_v.shape[0]):
        stiff_hi[i], stiff_lo[i] = split(stiff_v[i])

    def stacked(value):
        vh, vl = split(value)
        vh, vl = vh.astype(F32), vl.astype(F32)
        return jnp.concatenate([vh, vl, jnp.zeros((8, value.shape[1]), F32)], axis=0).astype(BF16)

    width = 3 * points
    group_rows = n * cols

    def couple(value, turn):
        lhs = stacked(value)
        total = jnp.zeros((group_rows, width), F32)
        row_at = lax.broadcasted_iota(I32, (group_rows, width), 0)
        col_at = lax.broadcasted_iota(I32, (cols, width), 0)
        for i in range(stiff_v.shape[0]):
            a = dot(lhs, stiff_hi[i], NT)
            b = dot(lhs, stiff_lo[i], NT)
            every = a[0:cols] + a[cols : 2 * cols] + b[0:cols]
            picked = jnp.sum(jnp.where(col_at == scol_ref[i], every, 0.0), axis=0, keepdims=True)
            total = total + jnp.where(row_at == srow_ref[i], picked, 0.0)
        for s in range(n):
            cpl_out[turn, s] = total[s * cols : (s + 1) * cols]
        copies = []
        for step in range(1, n):
            copies.append(
                pltpu.make_async_remote_copy(
                    src_ref=cpl_out.at[turn, lax.rem(x + step, n)],
                    dst_ref=cpl_in.at[turn, step - 1],
                    send_sem=cpl_send.at[turn, step - 1],
                    recv_sem=cpl_recv.at[turn, step - 1],
                    device_id=at(0, step),
                    device_id_type=MESH,
                )
            )
            copies[-1].start()
        return copies

    def coupled(turn, copies):
        total = cpl_out[turn, x]
        for step in range(1, n):
            copies[step - 1].wait_recv()
            total = total + cpl_in[turn, step - 1]
        return total

    field0 = jnp.concatenate([start_ref[c] for c in range(3)], axis=1)
    cpl_copies0 = couple(field0, 0)

    def phase_copies(group, phase, source, target, size):
        spans = (FIRST, REST)[group]
        copies = []
        for step in range(1, n):
            for part in range(3):
                axis = axes[part][phase]
                low_t, high_t = spans[part]
                to = lax.rem(place[axis] + step, n)
                if phase < 2:
                    src = source.at[low_t:high_t, pl.ds(pl.multiple_of(to * size, 8), size), :]
                else:
                    src = source.at[low_t:high_t, to]
                copies.append(
                    pltpu.make_async_remote_copy(
                        src_ref=src,
                        dst_ref=target.at[step - 1, low_t:high_t],
                        send_sem=axis_send.at[group, phase, part * (n - 1) + step - 1],
                        recv_sem=axis_recv.at[group, phase, part * (n - 1) + step - 1],
                        device_id=at(axis, step),
                        device_id_type=MESH,
                    )
                )
                copies[-1].start()
        return copies

    def phase_sum(group, phase, source, target, size, copies, put):
        for copy in copies:
            copy.wait_recv()
        for part in range(3):
            own = place[axes[part][phase]]
            for t in range(*(FIRST, REST)[group][part]):
                if phase < 2:
                    total = source[t, pl.ds(pl.multiple_of(own * size, 8), size), :]
                else:
                    total = source[t, own]
                for step in range(1, n):
                    total = total + target[step - 1, t]
                put(t, total)

    d_all, c_all = (d_first, d_rest), (c_first, c_rest)
    r1_all, f_all = (r1_first, r1_rest), (f_first, f_rest)
    r2_all, g_all = (r2_first, r2_rest), (g_first, g_rest)
    r3_all = (r3_first, r3_rest)
    done = []

    def stage0(group):
        core_copies[group].wait_recv()
        for t in range(c_all[group].shape[0]):
            c_all[group][t] = c_all[group][t] + d_all[group][t, pl.ds(pl.multiple_of(mine, 8), half), :]
        copies = phase_copies(group, 0, c_all[group], r1_all[group], rows1)
        done.extend(copies)
        return copies

    def stage1(group, copies):
        def put(t, total):
            f_all[group][t] = total

        phase_sum(group, 0, c_all[group], r1_all[group], rows1, copies, put)
        copies = phase_copies(group, 1, f_all[group], r2_all[group], rows2)
        done.extend(copies)
        return copies

    def stage2(group, copies):
        def put(t, total):
            for s in range(n):
                g_all[group][t, s] = total[s * cols : (s + 1) * cols]

        phase_sum(group, 1, f_all[group], r2_all[group], rows2, copies, put)
        copies = phase_copies(group, 2, g_all[group], r3_all[group], cols)
        done.extend(copies)
        return copies

    def stage3(group, copies):
        ends = {}

        def put(t, total):
            ends[t] = total

        phase_sum(group, 2, g_all[group], r3_all[group], cols, copies, put)
        return ends

    first = stage0(0)
    rest = stage0(1)
    first = stage1(0, first)

    loads[5].wait()
    for i in range(cols):
        inverse_hi[i], inverse_lo[i] = split(inverse_v[i])
    lane = lax.broadcasted_iota(I32, (blocks, keys), 1).astype(F32)
    flipped = codes[...].T
    for part in range(3):
        gather_hot[part] = jnp.where(lane == flipped[:, part : part + 1], 1.0, 0.0).astype(BF16)

    first = stage2(0, first)

    def correct(residual):
        lhs = stacked(residual)
        total = jnp.zeros((cols, width), F32)
        col_at = lax.broadcasted_iota(I32, (cols, width), 0)
        for k in range(cols):
            a = dot(lhs, inverse_hi[k], NT)
            b = dot(lhs, inverse_lo[k], NT)
            total = total + jnp.where(col_at == k, a[0:cols] + a[cols : 2 * cols] + b[0:cols], 0.0)
        return total

    ends = stage3(0, first)
    load = jnp.concatenate([ends[c] for c in range(3)], axis=1)
    field1 = field0 + correct(load - coupled(0, cpl_copies0))
    cpl_copies1 = couple(field1, 1)
    rest = stage1(1, rest)

    rows_s[...] = jnp.zeros_like(rows_s)
    for c in range(3):
        rows_s[c * cols : (c + 1) * cols, :] = field1[:, c * points : (c + 1) * points]
    uh, ul = split(rows_s[...])
    spread = dot(jnp.concatenate([uh, ul], axis=1), nt_w[...], NT) + dot(uh, nt_lo[...], NT)

    rest = stage2(1, rest)
    ends = stage3(1, rest)
    wide_s[...] = jnp.zeros_like(wide_s)
    for part in range(3):
        for j, p in enumerate(PART_W[part]):
            for c in range(3):
                wide_s[c * cols : (c + 1) * cols, p * points : (p + 1) * points] = ends[REST[part][0] + 1 + j]
    eh, el = split(spread * wide_s[...])
    back = dot(eh, nn_w[...]) + dot(el, nn_w[...])
    rows_s[...] = back[:, :points] + back[:, points:]
    load = jnp.concatenate(
        [ends[REST[c][0]] - rows_s[c * cols : (c + 1) * cols, :] for c in range(3)], axis=1
    )
    field2 = field1 + correct(load - coupled(1, cpl_copies1))

    for c in range(3):
        out_u[c] = field2[:, c * points : (c + 1) * points]
        gather3[c, place[axes[c][2]]] = field2[:, c * points : (c + 1) * points]

    def back_copies(phase, view):
        copies = []
        for step in range(1, n):
            for c in range(3):
                copies.append(
                    pltpu.make_async_remote_copy(
                        src_ref=view(c),
                        dst_ref=view(c),
                        send_sem=back_send.at[phase, c * (n - 1) + step - 1],
                        recv_sem=back_recv.at[phase, c * (n - 1) + step - 1],
                        device_id=at(axes[c][phase], step),
                        device_id_type=MESH,
                    )
                )
                copies[-1].start()
        done.extend(copies)
        return copies

    copies = back_copies(2, lambda c: gather3.at[c, place[axes[c][2]]])
    for copy in copies:
        copy.wait_recv()
    offset1 = [mine + place[axes[c][0]] * rows1 for c in range(3)]
    offset2 = [offset1[c] + place[axes[c][1]] * rows2 for c in range(3)]
    for c in range(3):
        whole = jnp.concatenate([gather3[c, s] for s in range(n)], axis=0)
        field[c, pl.ds(pl.multiple_of(offset2[c], 8), rows2), :] = whole
    copies = back_copies(1, lambda c: field.at[c, pl.ds(pl.multiple_of(offset2[c], 8), rows2), :])
    for copy in copies:
        copy.wait_recv()
    copies = back_copies(0, lambda c: field.at[c, pl.ds(pl.multiple_of(offset1[c], 8), rows1), :])
    for copy in copies:
        copy.wait_recv()
    homes = []
    for c in range(3):
        view = field.at[c, pl.ds(pl.multiple_of(mine, 8), half), :]
        homes.append(
            pltpu.make_async_remote_copy(
                src_ref=view,
                dst_ref=view,
                send_sem=home_send.at[c],
                recv_sem=home_recv.at[c],
                device_id=sibling,
                device_id_type=MESH,
            )
        )
        homes[-1].start()

    flipped = codes[...].T
    pattern_col = flipped[:, 3:4]
    for c in range(3):
        homes[c].wait_recv()
        fh, fl = split(field[c])
        got = dot(gather_hot[c], jnp.concatenate([fh, fl], axis=1)).astype(BF16)
        acc = jnp.zeros((blocks, points), F32)
        for j in range(patterns // 2):
            spot = slice(2 * j * points, 2 * (j + 1) * points)
            pair = dot(got, nt_w[spot, :], NT) + dot(got[:, :points], nt_lo[spot, :], NT)
            acc = jnp.where(pattern_col == 2 * j, pair[:, :points], acc)
            acc = jnp.where(pattern_col == 2 * j + 1, pair[:, points:], acc)
        out_i[c] = acc

    for copy in core_copies + cpl_copies0 + cpl_copies1 + done + homes:
        copy.wait_send()


def on_device(
    n,
    traction_base,
    added_mass,
    interface_prev,
    patch_route,
    basis_pattern,
    column_block,
    basis_values_table,
    stiffness,
    stiff_row,
    stiff_col,
    block_inverse,
    previous_shell_displacement,
):
    blocks = added_mass.shape[0]
    patterns, points, _ = basis_values_table.shape
    width = 3 * points
    cols = 4
    half, rows1, rows2 = n * n * n * cols, n * n * cols, n * cols
    keys = 2 * half
    stiffs = stiffness.shape[0]
    f, r = 3, 11
    any_, vmem, smem = (pl.BlockSpec(memory_space=m) for m in (pl.ANY, pltpu.VMEM, pltpu.SMEM))
    V = pltpu.VMEM
    dma = pltpu.SemaphoreType.DMA
    out_u, out_i = pl.pallas_call(
        functools.partial(kernel, n),
        out_shape=(
            jax.ShapeDtypeStruct((3, cols, points), F32),
            jax.ShapeDtypeStruct((3, blocks, points), F32),
        ),
        in_specs=[any_, any_, any_, vmem, vmem, vmem, any_, any_, smem, smem, any_, vmem],
        out_specs=(vmem, vmem),
        scratch_shapes=[
            V((3, blocks, points), F32),
            V((blocks, points), F32),
            V((3, blocks, points), F32),
            V((patterns, points, points), F32),
            V((stiffs, width, width), F32),
            V((cols, width, width), F32),
            V((stiffs, width, width), BF16),
            V((stiffs, width, width), BF16),
            V((cols, width, width), BF16),
            V((cols, width, width), BF16),
            V((patterns * points, 2 * points), BF16),
            V((patterns * points, 2 * points), BF16),
            V((patterns * points, points), BF16),
            V((128, blocks), F32),
            V((patterns, blocks, points), BF16),
            V((3, keys, blocks), BF16),
            V((3, blocks, keys), BF16),
            V((f, keys, points), F32),
            V((r, keys, points), F32),
            V((f, half, points), F32),
            V((r, half, points), F32),
            V((n - 1, f, rows1, points), F32),
            V((n - 1, r, rows1, points), F32),
            V((f, rows1, points), F32),
            V((r, rows1, points), F32),
            V((n - 1, f, rows2, points), F32),
            V((n - 1, r, rows2, points), F32),
            V((f, n, cols, points), F32),
            V((r, n, cols, points), F32),
            V((n - 1, f, cols, points), F32),
            V((n - 1, r, cols, points), F32),
            V((2, n, cols, width), F32),
            V((2, n - 1, cols, width), F32),
            V((16, points), F32),
            V((16, patterns * points), F32),
            V((3, n, cols, points), F32),
            V((3, keys, points), F32),
            dma((6,)),
            dma((2,)),
            dma((2,)),
            dma((2, 3, 3 * (n - 1))),
            dma((2, 3, 3 * (n - 1))),
            dma((2, n - 1)),
            dma((2, n - 1)),
            dma((3, 3 * (n - 1))),
            dma((3, 3 * (n - 1))),
            dma((3,)),
            dma((3,)),
        ],
        compiler_params=pltpu.CompilerParams(
            collective_id=0, has_side_effects=True, vmem_limit_bytes=62 * 1024 * 1024
        ),
    )(
        jnp.transpose(traction_base, (1, 0, 2)),
        added_mass,
        jnp.transpose(interface_prev, (1, 0, 2)),
        patch_route.reshape(1, blocks),
        basis_pattern.reshape(1, blocks),
        column_block.reshape(1, blocks),
        basis_values_table,
        stiffness,
        stiff_row,
        stiff_col,
        block_inverse,
        jnp.transpose(previous_shell_displacement, (1, 0, 2)),
    )
    return jnp.transpose(out_u, (1, 0, 2)), jnp.transpose(out_i, (1, 0, 2))


def solution(mesh):
    both = P(("fluid", "shell"))
    n = mesh.shape["shell"]
    return jax.shard_map(
        functools.partial(on_device, n),
        mesh=mesh,
        in_specs=(
            P(("fluid", "shell"), None, None),
            P(("fluid", "shell"), None),
            P(("fluid", "shell"), None, None),
            P(("fluid", "shell"), None),
            both,
            both,
            P(),
            P(("fluid", "shell"), None, None),
            both,
            both,
            P(("fluid", "shell"), None, None),
            P(("fluid", "shell"), None, None),
        ),
        out_specs=(P(("fluid", "shell"), None, None), P(("fluid", "shell"), None, None)),
        check_vma=False,
    )
```

time: 235 us -> 60.9 us (0.26)
  local copies, waits for them, and re-layouts: 75.8 us -> 3.05 us
  Pallas kernels: 0 us -> 56.9 us
  starting transfers between devices: 54 us -> 0 us
  waiting for transfers between devices: 43.2 us -> 0 us
  blocking collectives: 28.4 us -> 0 us
  matrix products: 23.4 us -> 0 us
  other arithmetic: 6.43 us -> 0 us
    pallas_call x0 -> x1, Pallas kernels: none -> 56.9 us  [on_device(): pl.pallas_call(functools.partial(kernel, n), out_shape=(jax.ShapeDtypeStr...]
    all_to_all x6 -> x0, starting transfers between devices: 54 us -> none  [the longest x2 23.1 us: on_device(): lax.all_to_all(replies, ('fluid', 'shell'), split_axis=0, concat_axis=0,...]
    scatter x4 -> x0, local copies, waits for them, and re-layouts: 51.8 us -> none  [the longest x2 48.7 us: on_device(): jnp.zeros((devices * capacity, 3, points), jnp.float32).at[slot_index]]
    all_to_all x6 -> x0, waiting for transfers between devices: 43.2 us -> none  [the longest x2 37.7 us: on_device(): lax.all_to_all(replies, ('fluid', 'shell'), split_axis=0, concat_axis=0,...]
    unnamed x2 -> x0, blocking collectives: 28.4 us -> none
    dot_general x12 -> x0, matrix products: 23.4 us -> none  [the longest x2 13.2 us: couple_rows(): jnp.einsum('bij,bj->bi', stiffness, flat_values[stiff_col], precision=lax...]
    gather x6 -> x0, local copies, waits for them, and re-layouts: 11.6 us -> none  [the longest x2 5.29 us: on_device(): replies = evaluated[jnp.maximum(codes, 0)]]
    all_to_all x4 -> x0, local copies, waits for them, and re-layouts: 6.3 us -> none  [the longest x2 4.84 us: on_device(): lax.all_to_all(outgoing, ('fluid', 'shell'), split_axis=0, concat_axis=0,...]
  transfers between devices with their start and end apart: 6 -> 0, of which waited for: 3 -> 0; matrix products, arithmetic and copies ran while one was open for 21% -> 0% of each run, Pallas kernels for 0% -> 0%
where the time goes in v1:
time: 60.9 us; the launch traced here: 60.6 us
  Pallas kernels  56.9 us (93%)
  local copies, waits for them, and re-layouts  3.05 us (5%)
  between operations  0.64 us (1%)
    pallas_call x1, Pallas kernels, on_device(): pl.pallas_call(functools.partial(kernel, n), out_shape=(jax.ShapeDtypeStr...  56.9 us
    unnamed x2, local copies, waits for them, and re-layouts  3.05 us

profile of v1, /device:TPU:1, one launch (start us, length us, event | category | flops | bytes accessed | tf_op | source)
XLA Modules:
  0.0 60.6 jit_solution(13201804774150805052)
XLA Ops:
  0.6 56.9 %shard_map.131 = (f32[3,4,128]{2,1,0:T(4,128)}, f32[3,256,128]{2,1,0:T(8,128)}) custom-call(f32[3,256,128]{2,1,0:T(8,128)} %bitcast.8, f32[256,128]{1,0:T(8,128)} %mass_h.1, f32[3,256,128]{2,1,0:T(8,128)} %bitcast.9, s32[1,256]{1,0:T(1,128)} %bitcast.13, s32[1,256]{1,0:T(1,128)} %bitcast.14, s32[1,256]{1,0:T(1,128)} %bitcast.15, f32[8,128,128]{2,1,0:T(8,128)} %table_h.1, ...), custom_call_target="tpu_custom_call" | custom-call | tf_op jit(solution)/shard_map/pallas_call | solution.py:492
  57.6 1.3 %copy.16 = f32[4,3,128]{2,0,1:T(4,128)} copy(f32[4,3,128]{2,0,1:T(4,128)} %bitcast.12) | data formatting | bytes 12288
  58.9 1.8 %copy.17 = f32[256,3,128]{2,0,1:T(8,128)} copy(f32[256,3,128]{2,0,1:T(8,128)} %bitcast.10) | data formatting | bytes 786432

commit v2 on v1

v2 whole, which is shorter than its diff:
```python
import functools

import jax
import jax.numpy as jnp
from jax import lax
from jax.experimental import pallas as pl
from jax.experimental.pallas import tpu as pltpu
from jax.sharding import PartitionSpec as P

F32, BF16, I32 = jnp.float32, jnp.bfloat16, jnp.int32
NT = (((1,), (1,)), ((), ()))
NN = (((1,), (0,)), ((), ()))
PART_W = ((0, 1, 2), (3, 4, 5), (6, 7))


def split(value):
    high = value.astype(BF16)
    low = (value - high.astype(F32)).astype(BF16)
    return high, low


def dot(a, b, dims=NN):
    return lax.dot_general(a, b, dims, preferred_element_type=F32)


def kernel(
    n,
    base_h,
    mass_h,
    prev_h,
    route_h,
    pattern_h,
    column_h,
    table_h,
    stiff_h,
    srow_h,
    scol_h,
    inverse_h,
    start_h,
    out_u,
    out_i,
    base_v,
    mass_v,
    prev_v,
    route_v,
    pattern_v,
    column_v,
    table_v,
    stiff_v,
    srow_s,
    scol_s,
    inverse_v,
    start_v,
    stiff_hi,
    stiff_lo,
    inverse_hi,
    inverse_lo,
    nn_w,
    nt_w,
    nt_lo,
    codes,
    pmask,
    scatter_hot,
    gather_hot,
    d_all,
    c_all,
    r1_all,
    f_first,
    f_rest,
    r2_first,
    r2_rest,
    cpl_out,
    cpl_in,
    rows_s,
    wide_s,
    field,
    load_sem,
    core_send,
    core_recv,
    axis_send,
    axis_recv,
    plane_send,
    plane_recv,
    cpl_send,
    cpl_recv,
    back_send,
    back_recv,
    home_send,
    home_recv,
):
    fluid, x = lax.axis_index("fluid"), lax.axis_index("shell")
    core = lax.rem(fluid, 2)
    y = lax.rem(lax.div(fluid, 2), n)
    z = lax.div(fluid, 2 * n)
    cols = 4
    half, rows1 = n * n * n * cols, n * n * cols
    blocks = mass_v.shape[0]
    patterns = table_v.shape[0]
    points = table_v.shape[1]
    keys = 2 * half
    chips = n * n * n
    width = 3 * points
    place = (x, y, z)
    axes = ((0, 1, 2), (1, 2, 0), (2, 0, 1))
    MESH = pl.DeviceIdType.MESH

    def shifted(dx, dy, dz):
        to_x, to_y, to_z = lax.rem(x + dx, n), lax.rem(y + dy, n), lax.rem(z + dz, n)
        return ((to_z * n + to_y) * 2 + core, to_x)

    def far(offsets):
        return sum(min(v, n - v) for v in offsets)

    everywhere = sorted(
        ((a, b, c) for c in range(n) for b in range(n) for a in range(n) if a or b or c),
        key=far,
        reverse=True,
    )
    sibling = (fluid + 1 - 2 * core, x)

    sources = (route_h, pattern_h, column_h, mass_h, prev_h, base_h, table_h, start_h, srow_h, scol_h, stiff_h, inverse_h)
    places = (route_v, pattern_v, column_v, mass_v, prev_v, base_v, table_v, start_v, srow_s, scol_s, stiff_v, inverse_v)
    names = ("route", "pattern", "column", "mass", "prev", "base", "table", "start", "srow", "scol", "stiff", "inverse")
    loads = {}
    for i, (name, src, dst) in enumerate(zip(names, sources, places)):
        loads[name] = pltpu.make_async_copy(src, dst, load_sem.at[i])
        loads[name].start()

    barrier = pltpu.get_barrier_semaphore()
    partners = [sibling] + [shifted(*o) for o in everywhere]
    for partner in partners:
        pl.semaphore_signal(barrier, inc=1, device_id=partner, device_id_type=MESH)

    for name in ("route", "pattern", "column"):
        loads[name].wait()
    route, column, pattern = route_v[...], column_v[...], pattern_v[...]
    bits = n.bit_length() - 1
    px = route & (n - 1)
    pcore = (route >> bits) & 1
    py = (route >> (bits + 1)) & (n - 1)
    pz = route >> (2 * bits + 1)
    where_is = (px, py, pz)
    code = [
        (((pcore * n + where_is[a]) * n + where_is[b]) * n + where_is[c]) * cols + column
        for a, b, c in axes
    ]
    codes[...] = jnp.zeros_like(codes)
    codes[0:1, :] = ((((pcore * n + pz) * n + py) * n + px) * cols + column).astype(F32)
    codes[1:2, :] = pattern.astype(F32)
    flipped = codes[...].T
    for p in range(patterns):
        pmask[p] = jnp.broadcast_to(jnp.where(flipped[:, 1:2] == p, 1.0, 0.0), (blocks, points)).astype(BF16)
    sub = lax.broadcasted_iota(I32, (keys, blocks), 0)
    for part in range(3):
        scatter_hot[part] = jnp.where(sub == code[part], 1.0, 0.0).astype(BF16)

    loads["table"].wait()
    for p in range(patterns):
        th, tl = split(table_v[p])
        spot = slice(p * points, (p + 1) * points)
        nn_w[spot, :points] = th
        nn_w[spot, points:] = tl
        nt_w[spot, :points] = th
        nt_w[spot, points:] = th
        nt_lo[spot, :] = tl

    def folded(pair):
        return pair[:, :points] + pair[:, points:]

    def project(values):
        parts = []
        for value in values:
            parts.extend(split(value))
        wide = jnp.concatenate(
            [jnp.concatenate([v * pmask[p] for v in parts], axis=0) for p in range(patterns)], axis=1
        )
        got = dot(wide, nn_w[...])
        ends = []
        for i in range(3):
            both = got[2 * i * blocks : (2 * i + 1) * blocks] + got[(2 * i + 1) * blocks : (2 * i + 2) * blocks]
            ends.append(jnp.concatenate(split(folded(both)), axis=1))
        return ends

    GROUPS = ((0, 3), (3, 3 + patterns), (3 + patterns, 6 + patterns))
    SPANS = (
        ((0, 1), (1, 2), (2, 3)),
        ((3, 6), (6, 9), (9, 11)),
        ((11, 12), (12, 13), (13, 14)),
    )
    other = pl.multiple_of((1 - core) * half, 8)
    mine = pl.multiple_of(core * half, 8)

    def to_sibling(group):
        low_t, high_t = GROUPS[group]
        copy = pltpu.make_async_remote_copy(
            src_ref=d_all.at[low_t:high_t, pl.ds(other, half), :],
            dst_ref=c_all.at[low_t:high_t],
            send_sem=core_send.at[group],
            recv_sem=core_recv.at[group],
            device_id=sibling,
            device_id_type=MESH,
        )
        copy.start()
        return copy

    done = []

    def stage0(group, copy):
        copy.wait_recv()
        done.append(copy)
        for t in range(*GROUPS[group]):
            c_all[t] = c_all[t] + d_all[t, pl.ds(mine, half), :]
        copies = []
        for step in range(1, n):
            for part in range(3):
                axis = axes[part][0]
                low_t, high_t = SPANS[group][part]
                to = lax.rem(place[axis] + step, n)
                slot = part * (n - 1) + step - 1
                target = shifted(*[step if a == axis else 0 for a in range(3)])
                copies.append(
                    pltpu.make_async_remote_copy(
                        src_ref=c_all.at[low_t:high_t, pl.ds(pl.multiple_of(to * rows1, 8), rows1), :],
                        dst_ref=r1_all.at[step - 1, low_t:high_t],
                        send_sem=axis_send.at[group, slot],
                        recv_sem=axis_recv.at[group, slot],
                        device_id=target,
                        device_id_type=MESH,
                    )
                )
                copies[-1].start()
        done.extend(copies)
        return copies

    loads["mass"].wait()
    loads["prev"].wait()
    loads["base"].wait()
    force = project([base_v[c] - mass_v[...] * prev_v[c] for c in range(3)])
    for c in range(3):
        d_all[c] = folded(dot(scatter_hot[c], force[c]))
    pl.semaphore_wait(barrier, len(partners))
    core0 = to_sibling(0)

    high, low = split(mass_v[...])
    for part in range(3):
        for j, p in enumerate(PART_W[part]):
            masked = jnp.concatenate([high * pmask[p], low * pmask[p]], axis=1)
            d_all[SPANS[1][part][0] + j] = folded(dot(scatter_hot[part], masked))
    core1 = to_sibling(1)
    axis0 = stage0(0, core0)
    load = project([base_v[c] for c in range(3)])
    for c in range(3):
        d_all[SPANS[2][c][0]] = folded(dot(scatter_hot[c], load[c]))
    core2 = to_sibling(2)
    axis1 = stage0(1, core1)
    axis2 = stage0(2, core2)

    loads["stiff"].wait()
    loads["srow"].wait()
    loads["scol"].wait()
    loads["start"].wait()
    for i in range(stiff_v.shape[0]):
        stiff_hi[i], stiff_lo[i] = split(stiff_v[i])

    def stacked(value):
        vh, vl = split(value)
        vh, vl = vh.astype(F32), vl.astype(F32)
        return jnp.concatenate([vh, vl, jnp.zeros((8, value.shape[1]), F32)], axis=0).astype(BF16)

    group_rows = n * cols

    def couple(value, turn):
        lhs = stacked(value)
        total = jnp.zeros((group_rows, width), F32)
        row_at = lax.broadcasted_iota(I32, (group_rows, width), 0)
        col_at = lax.broadcasted_iota(I32, (cols, width), 0)
        for i in range(stiff_v.shape[0]):
            a = dot(lhs, stiff_hi[i], NT)
            b = dot(lhs, stiff_lo[i], NT)
            every = a[0:cols] + a[cols : 2 * cols] + b[0:cols]
            picked = jnp.sum(jnp.where(col_at == scol_s[i], every, 0.0), axis=0, keepdims=True)
            total = total + jnp.where(row_at == srow_s[i], picked, 0.0)
        for s in range(n):
            cpl_out[turn, s] = total[s * cols : (s + 1) * cols]
        copies = []
        for step in range(1, n):
            copies.append(
                pltpu.make_async_remote_copy(
                    src_ref=cpl_out.at[turn, lax.rem(x + step, n)],
                    dst_ref=cpl_in.at[turn, step - 1],
                    send_sem=cpl_send.at[turn, step - 1],
                    recv_sem=cpl_recv.at[turn, step - 1],
                    device_id=shifted(step, 0, 0),
                    device_id_type=MESH,
                )
            )
            copies[-1].start()
        done.extend(copies)
        return copies

    def coupled(turn, copies):
        total = cpl_out[turn, x]
        for step in range(1, n):
            copies[step - 1].wait_recv()
            total = total + cpl_in[turn, step - 1]
        return total

    field0 = jnp.concatenate([start_v[c] for c in range(3)], axis=1)
    cpl_copies0 = couple(field0, 0)

    flat = sorted(((a, b) for a in range(n) for b in range(n) if a or b), key=far, reverse=True)

    def stage1(groups, copies, f_ref):
        for copy in copies:
            copy.wait_recv()
        for part in range(3):
            own = pl.multiple_of(place[axes[part][0]] * rows1, 8)
            at = 0
            for group in groups:
                for t in range(*SPANS[group][part]):
                    total = c_all[t, pl.ds(own, rows1), :]
                    for step in range(1, n):
                        total = total + r1_all[step - 1, t]
                    for s in range(n * n):
                        f_ref[part, s, at] = total[s * cols : (s + 1) * cols]
                    at += 1

    def plane(kind, f_ref, r_ref, counts):
        for i, (da, db) in enumerate(flat):
            for part in range(3):
                _, a, b = axes[part]
                to = lax.rem(place[a] + da, n) * n + lax.rem(place[b] + db, n)
                step = [0, 0, 0]
                step[a], step[b] = da, db
                pltpu.make_async_remote_copy(
                    src_ref=f_ref.at[part, to, 0 : counts[part]],
                    dst_ref=r_ref[part].at[i],
                    send_sem=plane_send.at[kind, part],
                    recv_sem=plane_recv.at[kind, part],
                    device_id=shifted(*step),
                    device_id_type=MESH,
                ).start()

    def all_of(ref, send, recv):
        return pltpu.make_async_remote_copy(
            src_ref=ref, dst_ref=ref, send_sem=send, recv_sem=recv, device_id=sibling, device_id_type=MESH
        )

    def plane_end(kind, f_ref, r_ref, counts):
        ends = []
        for part in range(3):
            copy = all_of(r_ref[part], plane_send.at[kind, part], plane_recv.at[kind, part])
            copy.wait_recv()
            done.append(copy)
            _, a, b = axes[part]
            own = place[a] * n + place[b]
            rows = []
            for t in range(counts[part]):
                total = f_ref[part, own, t]
                for i in range(len(flat)):
                    total = total + r_ref[part][i, t]
                rows.append(total)
            ends.append(rows)
        return ends

    one, rest = (1, 1, 1), tuple(len(PART_W[part]) + 1 for part in range(3))
    stage1((0,), axis0, f_first)
    plane(0, f_first, r2_first, one)

    loads["inverse"].wait()
    for i in range(cols):
        inverse_hi[i], inverse_lo[i] = split(inverse_v[i])
    flipped = codes[...].T
    lane = lax.broadcasted_iota(I32, (blocks, keys), 1).astype(F32)
    gather_hot[...] = jnp.where(lane == flipped[:, 0:1], 1.0, 0.0).astype(BF16)

    def correct(residual):
        lhs = stacked(residual)
        total = jnp.zeros((cols, width), F32)
        col_at = lax.broadcasted_iota(I32, (cols, width), 0)
        for k in range(cols):
            a = dot(lhs, inverse_hi[k], NT)
            b = dot(lhs, inverse_lo[k], NT)
            total = total + jnp.where(col_at == k, a[0:cols] + a[cols : 2 * cols] + b[0:cols], 0.0)
        return total

    stage1((2, 1), axis1 + axis2, f_rest)
    plane(1, f_rest, r2_rest, rest)
    ends = plane_end(0, f_first, r2_first, one)
    load = jnp.concatenate([ends[c][0] for c in range(3)], axis=1)
    field1 = field0 + correct(load - coupled(0, cpl_copies0))
    cpl_copies1 = couple(field1, 1)

    rows_s[...] = jnp.zeros_like(rows_s)
    for c in range(3):
        rows_s[c * cols : (c + 1) * cols, :] = field1[:, c * points : (c + 1) * points]
    uh, ul = split(rows_s[...])
    spread = dot(jnp.concatenate([uh, ul], axis=1), nt_w[...], NT) + dot(uh, nt_lo[...], NT)

    ends = plane_end(1, f_rest, r2_rest, rest)
    wide_s[...] = jnp.zeros_like(wide_s)
    for part in range(3):
        for j, p in enumerate(PART_W[part]):
            for c in range(3):
                wide_s[c * cols : (c + 1) * cols, p * points : (p + 1) * points] = ends[part][1 + j]
    eh, el = split(spread * wide_s[...])
    rows_s[...] = folded(dot(eh, nn_w[...]) + dot(el, nn_w[...]))
    load = jnp.concatenate([ends[c][0] - rows_s[c * cols : (c + 1) * cols, :] for c in range(3)], axis=1)
    field2 = field1 + correct(load - coupled(1, cpl_copies1))

    for c in range(3):
        out_u[c] = field2[:, c * points : (c + 1) * points]
    chip = (z * n + y) * n + x
    home = pl.multiple_of(core * chips, 8)
    field[home + chip] = field2
    for offsets in everywhere:
        pltpu.make_async_remote_copy(
            src_ref=field.at[home + chip],
            dst_ref=field.at[home + chip],
            send_sem=back_send,
            recv_sem=back_recv,
            device_id=shifted(*offsets),
            device_id_type=MESH,
        ).start()
    copy = all_of(field.at[pl.ds(home, chips - 1)], back_send, back_recv)
    copy.wait_recv()
    done.append(copy)
    view = field.at[pl.ds(home, chips)]
    copy = pltpu.make_async_remote_copy(
        src_ref=view,
        dst_ref=view,
        send_sem=home_send,
        recv_sem=home_recv,
        device_id=sibling,
        device_id_type=MESH,
    )
    copy.start()
    copy.wait_recv()
    done.append(copy)

    flipped = codes[...].T
    pattern_col = flipped[:, 1:2]
    fh, fl = split(field[...].reshape(keys, width))
    rows = []
    for c in range(3):
        spot = slice(c * points, (c + 1) * points)
        rows.append(dot(gather_hot[...], jnp.concatenate([fh[:, spot], fl[:, spot]], axis=1)).astype(BF16))
    got = jnp.concatenate(rows, axis=0)
    acc = [jnp.zeros((blocks, points), F32) for _ in range(3)]
    for j in range(patterns // 2):
        spot = slice(2 * j * points, 2 * (j + 1) * points)
        pair = dot(got, nt_w[spot, :], NT) + dot(got[:, :points], nt_lo[spot, :], NT)
        for c in range(3):
            mid = pair[c * blocks : (c + 1) * blocks]
            acc[c] = jnp.where(pattern_col == 2 * j, mid[:, :points], acc[c])
            acc[c] = jnp.where(pattern_col == 2 * j + 1, mid[:, points:], acc[c])
    for c in range(3):
        out_i[c] = acc[c]

    for copy in done:
        copy.wait_send()


def on_device(
    n,
    traction_base,
    added_mass,
    interface_prev,
    patch_route,
    basis_pattern,
    column_block,
    basis_values_table,
    stiffness,
    stiff_row,
    stiff_col,
    block_inverse,
    previous_shell_displacement,
):
    blocks = added_mass.shape[0]
    patterns, points, _ = basis_values_table.shape
    width = 3 * points
    cols = 4
    chips = n * n * n
    half, rows1 = chips * cols, n * n * cols
    keys = 2 * half
    stiffs = stiffness.shape[0]
    total = 6 + patterns
    any_, vmem = (pl.BlockSpec(memory_space=m) for m in (pl.ANY, pltpu.VMEM))
    V = pltpu.VMEM
    dma = pltpu.SemaphoreType.DMA
    rest = [len(p) + 1 for p in PART_W]
    out_u, out_i = pl.pallas_call(
        functools.partial(kernel, n),
        out_shape=(
            jax.ShapeDtypeStruct((3, cols, points), F32),
            jax.ShapeDtypeStruct((3, blocks, points), F32),
        ),
        in_specs=[any_] * 12,
        out_specs=(vmem, vmem),
        scratch_shapes=[
            V((3, blocks, points), F32),
            V((blocks, points), F32),
            V((3, blocks, points), F32),
            V((1, blocks), I32),
            V((1, blocks), I32),
            V((1, blocks), I32),
            V((patterns, points, points), F32),
            V((stiffs, width, width), F32),
            pltpu.SMEM((stiffs,), I32),
            pltpu.SMEM((stiffs,), I32),
            V((cols, width, width), F32),
            V((3, cols, points), F32),
            V((stiffs, width, width), BF16),
            V((stiffs, width, width), BF16),
            V((cols, width, width), BF16),
            V((cols, width, width), BF16),
            V((patterns * points, 2 * points), BF16),
            V((patterns * points, 2 * points), BF16),
            V((patterns * points, points), BF16),
            V((128, blocks), F32),
            V((patterns, blocks, points), BF16),
            V((3, keys, blocks), BF16),
            V((blocks, keys), BF16),
            V((total, keys, points), F32),
            V((total, half, points), F32),
            V((n - 1, total, rows1, points), F32),
            V((3, n * n, 1, cols, points), F32),
            V((3, n * n, max(rest), cols, points), F32),
            [V((n * n - 1, 1, cols, points), F32) for _ in range(3)],
            [V((n * n - 1, rest[part], cols, points), F32) for part in range(3)],
            V((2, n, cols, width), F32),
            V((2, n - 1, cols, width), F32),
            V((16, points), F32),
            V((16, patterns * points), F32),
            V((2 * chips, cols, width), F32),
            dma((12,)),
            dma((3,)),
            dma((3,)),
            dma((3, 3 * (n - 1))),
            dma((3, 3 * (n - 1))),
            dma((2, 3)),
            dma((2, 3)),
            dma((2, n - 1)),
            dma((2, n - 1)),
            dma,
            dma,
            dma,
            dma,
        ],
        compiler_params=pltpu.CompilerParams(
            collective_id=0, has_side_effects=True, vmem_limit_bytes=62 * 1024 * 1024
        ),
    )(
        jnp.transpose(traction_base, (1, 0, 2)),
        added_mass,
        jnp.transpose(interface_prev, (1, 0, 2)),
        patch_route.reshape(1, blocks),
        basis_pattern.reshape(1, blocks),
        column_block.reshape(1, blocks),
        basis_values_table,
        stiffness,
        stiff_row,
        stiff_col,
        block_inverse,
        jnp.transpose(previous_shell_displacement, (1, 0, 2)),
    )
    return jnp.transpose(out_u, (1, 0, 2)), jnp.transpose(out_i, (1, 0, 2))


def solution(mesh):
    both = P(("fluid", "shell"))
    n = mesh.shape["shell"]
    return jax.shard_map(
        functools.partial(on_device, n),
        mesh=mesh,
        in_specs=(
            P(("fluid", "shell"), None, None),
            P(("fluid", "shell"), None),
            P(("fluid", "shell"), None, None),
            P(("fluid", "shell"), None),
            both,
            both,
            P(),
            P(("fluid", "shell"), None, None),
            both,
            both,
            P(("fluid", "shell"), None, None),
            P(("fluid", "shell"), None, None),
        ),
        out_specs=(P(("fluid", "shell"), None, None), P(("fluid", "shell"), None, None)),
        check_vma=False,
    )
```

time: 60.9 us -> 46 us (0.76)
  Pallas kernels: 56.9 us -> 42.1 us
    pallas_call x1, Pallas kernels: 56.9 us -> 42.1 us  [on_device(): pl.pallas_call(functools.partial(kernel, n), out_shape=(jax.ShapeDtypeStr...]
where the time goes in v2:
time: 46 us; the launch traced here: 45.8 us
  Pallas kernels  42.1 us (92%)
  local copies, waits for them, and re-layouts  3.05 us (7%)
  between operations  0.64 us (1%)
    pallas_call x1, Pallas kernels, on_device(): pl.pallas_call(functools.partial(kernel, n), out_shape=(jax.ShapeDtypeStr...  42.1 us
    unnamed x2, local copies, waits for them, and re-layouts  3.05 us

profile of v2, /device:TPU:1, one launch (start us, length us, event | category | flops | bytes accessed | tf_op | source)
XLA Modules:
  0.0 45.8 jit_solution(12753815412324248537)
XLA Ops:
  0.6 42.1 %shard_map.131 = (f32[3,4,128]{2,1,0:T(4,128)}, f32[3,256,128]{2,1,0:T(8,128)}) custom-call(f32[3,256,128]{2,1,0:T(8,128)} %bitcast.8, f32[256,128]{1,0:T(8,128)} %mass_h.1, f32[3,256,128]{2,1,0:T(8,128)} %bitcast.9, s32[1,256]{1,0:T(1,128)} %bitcast.13, s32[1,256]{1,0:T(1,128)} %bitcast.14, s32[1,256]{1,0:T(1,128)} %bitcast.15, f32[8,128,128]{2,1,0:T(8,128)} %table_h.1, ...), custom_call_target="tpu_custom_call" | custom-call | tf_op jit(solution)/shard_map/pallas_call | solution.py:492
  42.8 1.3 %copy.16 = f32[4,3,128]{2,0,1:T(4,128)} copy(f32[4,3,128]{2,0,1:T(4,128)} %bitcast.12) | data formatting | bytes 12288
  44.0 1.8 %copy.17 = f32[256,3,128]{2,0,1:T(8,128)} copy(f32[256,3,128]{2,0,1:T(8,128)} %bitcast.10) | data formatting | bytes 786432

commit v3 on v2

--- a/solution.py
+++ b/solution.py
@@ -10,9 +10,6 @@
 F32, BF16, I32 = jnp.float32, jnp.bfloat16, jnp.int32
 NT = (((1,), (1,)), ((), ()))
 NN = (((1,), (0,)), ((), ()))
-PART_W = ((0, 1, 2), (3, 4, 5), (6, 7))
-
-
 def split(value):
     high = value.astype(BF16)
     low = (value - high.astype(F32)).astype(BF16)
@@ -65,10 +62,11 @@
     d_all,
     c_all,
     r1_all,
-    f_first,
-    f_rest,
-    r2_first,
-    r2_rest,
+    f_all,
+    r2_all,
+    slot_own,
+    slot_out,
+    slot_in,
     cpl_out,
     cpl_in,
     rows_s,
@@ -81,6 +79,8 @@
     axis_recv,
     plane_send,
     plane_recv,
+    slot_send,
+    slot_recv,
     cpl_send,
     cpl_recv,
     back_send,
@@ -100,6 +100,8 @@
     keys = 2 * half
     chips = n * n * n
     width = 3 * points
+    cap = 4
+    tags = patterns * cols
     place = (x, y, z)
     axes = ((0, 1, 2), (1, 2, 0), (2, 0, 1))
     MESH = pl.DeviceIdType.MESH
@@ -147,6 +149,8 @@
     codes[...] = jnp.zeros_like(codes)
     codes[0:1, :] = ((((pcore * n + pz) * n + py) * n + px) * cols + column).astype(F32)
     codes[1:2, :] = pattern.astype(F32)
+    codes[2:3, :] = (((pcore * n + pz) * n + py) * n + px).astype(F32)
+    codes[3:4, :] = (pattern * cols + column).astype(F32)
     flipped = codes[...].T
     for p in range(patterns):
         pmask[p] = jnp.broadcast_to(jnp.where(flipped[:, 1:2] == p, 1.0, 0.0), (blocks, points)).astype(BF16)
@@ -181,17 +185,11 @@
             ends.append(jnp.concatenate(split(folded(both)), axis=1))
         return ends
 
-    GROUPS = ((0, 3), (3, 3 + patterns), (3 + patterns, 6 + patterns))
-    SPANS = (
-        ((0, 1), (1, 2), (2, 3)),
-        ((3, 6), (6, 9), (9, 11)),
-        ((11, 12), (12, 13), (13, 14)),
-    )
     other = pl.multiple_of((1 - core) * half, 8)
     mine = pl.multiple_of(core * half, 8)
 
     def to_sibling(group):
-        low_t, high_t = GROUPS[group]
+        low_t, high_t = 3 * group, 3 * group + 3
         copy = pltpu.make_async_remote_copy(
             src_ref=d_all.at[low_t:high_t, pl.ds(other, half), :],
             dst_ref=c_all.at[low_t:high_t],
@@ -208,20 +206,20 @@
     def stage0(group, copy):
         copy.wait_recv()
         done.append(copy)
-        for t in range(*GROUPS[group]):
+        for t in range(3 * group, 3 * group + 3):
             c_all[t] = c_all[t] + d_all[t, pl.ds(mine, half), :]
         copies = []
         for step in range(1, n):
             for part in range(3):
                 axis = axes[part][0]
-                low_t, high_t = SPANS[group][part]
+                t = 3 * group + part
                 to = lax.rem(place[axis] + step, n)
                 slot = part * (n - 1) + step - 1
                 target = shifted(*[step if a == axis else 0 for a in range(3)])
                 copies.append(
                     pltpu.make_async_remote_copy(
-                        src_ref=c_all.at[low_t:high_t, pl.ds(pl.multiple_of(to * rows1, 8), rows1), :],
-                        dst_ref=r1_all.at[step - 1, low_t:high_t],
+                        src_ref=c_all.at[t, pl.ds(pl.multiple_of(to * rows1, 8), rows1), :],
+                        dst_ref=r1_all.at[step - 1, t],
                         send_sem=axis_send.at[group, slot],
                         recv_sem=axis_recv.at[group, slot],
                         device_id=target,
@@ -241,26 +239,112 @@
     pl.semaphore_wait(barrier, len(partners))
     core0 = to_sibling(0)
 
-    high, low = split(mass_v[...])
-    for part in range(3):
-        for j, p in enumerate(PART_W[part]):
-            masked = jnp.concatenate([high * pmask[p], low * pmask[p]], axis=1)
-            d_all[SPANS[1][part][0] + j] = folded(dot(scatter_hot[part], masked))
-    core1 = to_sibling(1)
+    owner_col = lax.broadcast_in_dim(flipped[:, 2:3], (blocks, blocks), (0, 1))
+    same = owner_col == codes[2:3, :]
+    down = lax.broadcasted_iota(I32, (blocks, blocks), 0)
+    along = lax.broadcasted_iota(I32, (blocks, blocks), 1)
+    slot_row = jnp.sum(jnp.where(same & (down < along), 1.0, 0.0), axis=0, keepdims=True)
+    slot_col = jnp.sum(jnp.where(same & (along < down), 1.0, 0.0), axis=1, keepdims=True)
+    owners = 2 * chips
+    spot_of = slot_row * owners + codes[2:3, :]
+    hot = jnp.where(lax.broadcasted_iota(I32, (cap * owners, blocks), 0).astype(F32) == spot_of, 1.0, 0.0).astype(BF16)
+    slots = folded(dot(hot, jnp.concatenate(split(mass_v[...]), axis=1)))
+    mark = slot_col * tags + flipped[:, 3:4]
+    marked = jnp.where(lax.broadcasted_iota(I32, (blocks, points), 1).astype(F32) == mark, 1.0, 0.0).astype(BF16)
+    owner_hot = jnp.where(lax.broadcasted_iota(I32, (owners, blocks), 0).astype(F32) == codes[2:3, :], 1.0, 0.0).astype(BF16)
+    marks = dot(owner_hot, marked)
+    for s in range(2):
+        for j in range(cap):
+            slot_own[s, :, j, :] = slots[j * owners + s * chips : j * owners + (s + 1) * chips]
+        slot_own[s, :, cap, :] = marks[s * chips : (s + 1) * chips]
+    slot_copy = pltpu.make_async_remote_copy(
+        src_ref=slot_own.at[1 - core],
+        dst_ref=slot_out.at[core],
+        send_sem=core_send.at[2],
+        recv_sem=core_recv.at[2],
+        device_id=sibling,
+        device_id_type=MESH,
+    )
+    slot_copy.start()
+    slot_out[core] = slot_own[core]
+    chip = (z * n + y) * n + x
     axis0 = stage0(0, core0)
     load = project([base_v[c] for c in range(3)])
     for c in range(3):
-        d_all[SPANS[2][c][0]] = folded(dot(scatter_hot[c], load[c]))
-    core2 = to_sibling(2)
-    axis1 = stage0(1, core1)
-    axis2 = stage0(2, core2)
+        d_all[3 + c] = folded(dot(scatter_hot[c], load[c]))
+    core1 = to_sibling(1)
+    slot_copy.wait_recv()
+    done.append(slot_copy)
+    slot_in[:, chip] = slot_out[:, chip]
+    for dx, dy, dz in everywhere:
+        to = (lax.rem(z + dz, n) * n + lax.rem(y + dy, n)) * n + lax.rem(x + dx, n)
+        pltpu.make_async_remote_copy(
+            src_ref=slot_out.at[:, to],
+            dst_ref=slot_in.at[:, chip],
+            send_sem=slot_send,
+            recv_sem=slot_recv,
+            device_id=shifted(dx, dy, dz),
+            device_id_type=MESH,
+        ).start()
 
     loads["stiff"].wait()
     loads["srow"].wait()
     loads["scol"].wait()
     loads["start"].wait()
     for i in range(stiff_v.shape[0]):
-        stiff_hi[i], stiff_lo[i] = split(stiff_v[i])
+        stiff_hi[i], stiff_lo[i] = split(stiff_v[i].T)
+
+    axis1 = stage0(1, core1)
+
+    flat = sorted(((a, b) for a in range(n) for b in range(n) if a or b), key=far, reverse=True)
+
+    def stage1(group, copies):
+        for copy in copies:
+            copy.wait_recv()
+        for part in range(3):
+            own = pl.multiple_of(place[axes[part][0]] * rows1, 8)
+            t = 3 * group + part
+            total = c_all[t, pl.ds(own, rows1), :]
+            for step in range(1, n):
+                total = total + r1_all[step - 1, t]
+            for s in range(n * n):
+                f_all[t, s] = total[s * cols : (s + 1) * cols]
+        for i, (da, db) in enumerate(flat):
+            for part in range(3):
+                _, a, b = axes[part]
+                to = lax.rem(place[a] + da, n) * n + lax.rem(place[b] + db, n)
+                step = [0, 0, 0]
+                step[a], step[b] = da, db
+                t = 3 * group + part
+                pltpu.make_async_remote_copy(
+                    src_ref=f_all.at[t, to],
+                    dst_ref=r2_all.at[t, i],
+                    send_sem=plane_send.at[group],
+                    recv_sem=plane_recv.at[group],
+                    device_id=shifted(*step),
+                    device_id_type=MESH,
+                ).start()
+
+    def all_of(ref, send, recv):
+        return pltpu.make_async_remote_copy(
+            src_ref=ref, dst_ref=ref, send_sem=send, recv_sem=recv, device_id=sibling, device_id_type=MESH
+        )
+
+    def plane_end(group):
+        copy = all_of(r2_all.at[3 * group : 3 * group + 3], plane_send.at[group], plane_recv.at[group])
+        copy.wait_recv()
+        done.append(copy)
+        ends = []
+        for part in range(3):
+            _, a, b = axes[part]
+            t = 3 * group + part
+            total = f_all[t, place[a] * n + place[b]]
+            for i in range(len(flat)):
+                total = total + r2_all[t, i]
+            ends.append(total)
+        return jnp.concatenate(ends, axis=1)
+
+    stage1(0, axis0)
 
     def stacked(value):
         vh, vl = split(value)
@@ -275,8 +359,8 @@
         row_at = lax.broadcasted_iota(I32, (group_rows, width), 0)
         col_at = lax.broadcasted_iota(I32, (cols, width), 0)
         for i in range(stiff_v.shape[0]):
-            a = dot(lhs, stiff_hi[i], NT)
-            b = dot(lhs, stiff_lo[i], NT)
+            a = dot(lhs, stiff_hi[i])
+            b = dot(lhs, stiff_lo[i])
             every = a[0:cols] + a[cols : 2 * cols] + b[0:cols]
             picked = jnp.sum(jnp.where(col_at == scol_s[i], every, 0.0), axis=0, keepdims=True)
             total = total + jnp.where(row_at == srow_s[i], picked, 0.0)
@@ -308,68 +392,9 @@
     field0 = jnp.concatenate([start_v[c] for c in range(3)], axis=1)
     cpl_copies0 = couple(field0, 0)
 
-    flat = sorted(((a, b) for a in range(n) for b in range(n) if a or b), key=far, reverse=True)
-
-    def stage1(groups, copies, f_ref):
-        for copy in copies:
-            copy.wait_recv()
-        for part in range(3):
-            own = pl.multiple_of(place[axes[part][0]] * rows1, 8)
-            at = 0
-            for group in groups:
-                for t in range(*SPANS[group][part]):
-                    total = c_all[t, pl.ds(own, rows1), :]
-                    for step in range(1, n):
-                        total = total + r1_all[step - 1, t]
-                    for s in range(n * n):
-                        f_ref[part, s, at] = total[s * cols : (s + 1) * cols]
-                    at += 1
-
-    def plane(kind, f_ref, r_ref, counts):
-        for i, (da, db) in enumerate(flat):
-            for part in range(3):
-                _, a, b = axes[part]
-                to = lax.rem(place[a] + da, n) * n + lax.rem(place[b] + db, n)
-                step = [0, 0, 0]
-                step[a], step[b] = da, db
-                pltpu.make_async_remote_copy(
-                    src_ref=f_ref.at[part, to, 0 : counts[part]],
-                    dst_ref=r_ref[part].at[i],
-                    send_sem=plane_send.at[kind, part],
-                    recv_sem=plane_recv.at[kind, part],
-                    device_id=shifted(*step),
-                    device_id_type=MESH,
-                ).start()
-
-    def all_of(ref, send, recv):
-        return pltpu.make_async_remote_copy(
-            src_ref=ref, dst_ref=ref, send_sem=send, recv_sem=recv, device_id=sibling, device_id_type=MESH
-        )
-
-    def plane_end(kind, f_ref, r_ref, counts):
-        ends = []
-        for part in range(3):
-            copy = all_of(r_ref[part], plane_send.at[kind, part], plane_recv.at[kind, part])
-            copy.wait_recv()
-            done.append(copy)
-            _, a, b = axes[part]
-            own = place[a] * n + place[b]
-            rows = []
-            for t in range(counts[part]):
-                total = f_ref[part, own, t]
-                for i in range(len(flat)):
-                    total = total + r_ref[part][i, t]
-                rows.append(total)
-            ends.append(rows)
-        return ends
-
-    one, rest = (1, 1, 1), tuple(len(PART_W[part]) + 1 for part in range(3))
-    stage1((0,), axis0, f_first)
-    plane(0, f_first, r2_first, one)
-
     loads["inverse"].wait()
     for i in range(cols):
-        inverse_hi[i], inverse_lo[i] = split(inverse_v[i])
+        inverse_hi[i], inverse_lo[i] = split(inverse_v[i].T)
     flipped = codes[...].T
     lane = lax.broadcasted_iota(I32, (blocks, keys), 1).astype(F32)
     gather_hot[...] = jnp.where(lane == flipped[:, 0:1], 1.0, 0.0).astype(BF16)
@@ -379,16 +404,13 @@
         total = jnp.zeros((cols, width), F32)
         col_at = lax.broadcasted_iota(I32, (cols, width), 0)
         for k in range(cols):
-            a = dot(lhs, inverse_hi[k], NT)
-            b = dot(lhs, inverse_lo[k], NT)
+            a = dot(lhs, inverse_hi[k])
+            b = dot(lhs, inverse_lo[k])
             total = total + jnp.where(col_at == k, a[0:cols] + a[cols : 2 * cols] + b[0:cols], 0.0)
         return total
 
-    stage1((2, 1), axis1 + axis2, f_rest)
-    plane(1, f_rest, r2_rest, rest)
-    ends = plane_end(0, f_first, r2_first, one)
-    load = jnp.concatenate([ends[c][0] for c in range(3)], axis=1)
-    field1 = field0 + correct(load - coupled(0, cpl_copies0))
+    stage1(1, axis1)
+    field1 = field0 + correct(plane_end(0) - coupled(0, cpl_copies0))
     cpl_copies1 = couple(field1, 1)
 
     rows_s[...] = jnp.zeros_like(rows_s)
@@ -397,20 +419,29 @@
     uh, ul = split(rows_s[...])
     spread = dot(jnp.concatenate([uh, ul], axis=1), nt_w[...], NT) + dot(uh, nt_lo[...], NT)
 
-    ends = plane_end(1, f_rest, r2_rest, rest)
+    arrived = all_of(slot_in.at[:, pl.ds(0, chips - 1)], slot_send, slot_recv)
+    arrived.wait_recv()
+    done.append(arrived)
+    marks = jnp.concatenate([slot_in[s, :, cap, :] for s in range(2)], axis=0).T
+    summed = None
+    for j in range(cap):
+        values = jnp.concatenate([slot_in[s, :, j, :] for s in range(2)], axis=0)
+        got = dot(
+            marks[j * tags : (j + 1) * tags].astype(BF16), jnp.concatenate(split(values), axis=1)
+        )
+        summed = got if summed is None else summed + got
+    summed = folded(summed)
     wide_s[...] = jnp.zeros_like(wide_s)
-    for part in range(3):
-        for j, p in enumerate(PART_W[part]):
-            for c in range(3):
-                wide_s[c * cols : (c + 1) * cols, p * points : (p + 1) * points] = ends[part][1 + j]
+    for p in range(patterns):
+        for c in range(3):
+            wide_s[c * cols : (c + 1) * cols, p * points : (p + 1) * points] = summed[p * cols : (p + 1) * cols]
     eh, el = split(spread * wide_s[...])
     rows_s[...] = folded(dot(eh, nn_w[...]) + dot(el, nn_w[...]))
-    load = jnp.concatenate([ends[c][0] - rows_s[c * cols : (c + 1) * cols, :] for c in range(3)], axis=1)
+    load = plane_end(1) - jnp.concatenate([rows_s[c * cols : (c + 1) * cols, :] for c in range(3)], axis=1)
     field2 = field1 + correct(load - coupled(1, cpl_copies1))
 
     for c in range(3):
         out_u[c] = field2[:, c * points : (c + 1) * points]
-    chip = (z * n + y) * n + x
     home = pl.multiple_of(core * chips, 8)
     field[home + chip] = field2
     for offsets in everywhere:
@@ -484,11 +515,9 @@
     half, rows1 = chips * cols, n * n * cols
     keys = 2 * half
     stiffs = stiffness.shape[0]
-    total = 6 + patterns
     any_, vmem = (pl.BlockSpec(memory_space=m) for m in (pl.ANY, pltpu.VMEM))
     V = pltpu.VMEM
     dma = pltpu.SemaphoreType.DMA
-    rest = [len(p) + 1 for p in PART_W]
     out_u, out_i = pl.pallas_call(
         functools.partial(kernel, n),
         out_shape=(
@@ -521,13 +550,14 @@
             V((patterns, blocks, points), BF16),
             V((3, keys, blocks), BF16),
             V((blocks, keys), BF16),
-            V((total, keys, points), F32),
-            V((total, half, points), F32),
-            V((n - 1, total, rows1, points), F32),
-            V((3, n * n, 1, cols, points), F32),
-            V((3, n * n, max(rest), cols, points), F32),
-            [V((n * n - 1, 1, cols, points), F32) for _ in range(3)],
-            [V((n * n - 1, rest[part], cols, points), F32) for part in range(3)],
+            V((6, keys, points), F32),
+            V((6, half, points), F32),
+            V((n - 1, 6, rows1, points), F32),
+            V((6, n * n, cols, points), F32),
+            V((6, n * n - 1, cols, points), F32),
+            V((2, chips, 5, points), F32),
+            V((2, chips, 5, points), F32),
+            V((2, chips, 5, points), F32),
             V((2, n, cols, width), F32),
             V((2, n - 1, cols, width), F32),
             V((16, points), F32),
@@ -536,10 +566,12 @@
             dma((12,)),
             dma((3,)),
             dma((3,)),
-            dma((3, 3 * (n - 1))),
-            dma((3, 3 * (n - 1))),
-            dma((2, 3)),
-            dma((2, 3)),
+            dma((2, 3 * (n - 1))),
+            dma((2, 3 * (n - 1))),
+            dma((2,)),
+            dma((2,)),
+            dma,
+            dma,
             dma((2, n - 1)),
             dma((2, n - 1)),
             dma,

time: 46 us -> 43.7 us (0.950)
  Pallas kernels: 42.1 us -> 39.8 us
    pallas_call x1, Pallas kernels: 42.1 us -> 39.8 us  [on_device(): pl.pallas_call(functools.partial(kernel, n), out_shape=(jax.ShapeDtypeStr...]
where the time goes in v3:
time: 43.7 us; the launch traced here: 43.5 us
  Pallas kernels  39.8 us (91%)
  local copies, waits for them, and re-layouts  3.05 us (7%)
  between operations  0.64 us (1%)
    pallas_call x1, Pallas kernels, on_device(): pl.pallas_call(functools.partial(kernel, n), out_shape=(jax.ShapeDtypeStr...  39.8 us
    unnamed x2, local copies, waits for them, and re-layouts  3.05 us

profile of v3, /device:TPU:1, one launch (start us, length us, event | category | flops | bytes accessed | tf_op | source)
XLA Modules:
  0.0 43.5 jit_solution(11869939752805526482)
XLA Ops:
  0.6 39.8 %shard_map.131 = (f32[3,4,128]{2,1,0:T(4,128)}, f32[3,256,128]{2,1,0:T(8,128)}) custom-call(f32[3,256,128]{2,1,0:T(8,128)} %bitcast.8, f32[256,128]{1,0:T(8,128)} %mass_h.1, f32[3,256,128]{2,1,0:T(8,128)} %bitcast.9, s32[1,256]{1,0:T(1,128)} %bitcast.13, s32[1,256]{1,0:T(1,128)} %bitcast.14, s32[1,256]{1,0:T(1,128)} %bitcast.15, f32[8,128,128]{2,1,0:T(8,128)} %table_h.1, ...), custom_call_target="tpu_custom_call" | custom-call | tf_op jit(solution)/shard_map/pallas_call | solution.py:521
  40.4 1.3 %copy.16 = f32[4,3,128]{2,0,1:T(4,128)} copy(f32[4,3,128]{2,0,1:T(4,128)} %bitcast.12) | data formatting | bytes 12288
  41.7 1.8 %copy.17 = f32[256,3,128]{2,0,1:T(8,128)} copy(f32[256,3,128]{2,0,1:T(8,128)} %bitcast.10) | data formatting | bytes 786432

commit v4 on v3

--- a/solution.py
+++ b/solution.py
@@ -133,6 +133,9 @@
     for partner in partners:
         pl.semaphore_signal(barrier, inc=1, device_id=partner, device_id_type=MESH)
 
+    def folded(pair):
+        return pair[:, :points] + pair[:, points:]
+
     for name in ("route", "pattern", "column"):
         loads[name].wait()
     route, column, pattern = route_v[...], column_v[...], pattern_v[...]
@@ -158,18 +161,32 @@
     for part in range(3):
         scatter_hot[part] = jnp.where(sub == code[part], 1.0, 0.0).astype(BF16)
 
+    loads["mass"].wait()
+    owner_col = lax.broadcast_in_dim(flipped[:, 2:3], (blocks, blocks), (0, 1))
+    same = owner_col == codes[2:3, :]
+    down = lax.broadcasted_iota(I32, (blocks, blocks), 0)
+    along = lax.broadcasted_iota(I32, (blocks, blocks), 1)
+    slot_row = jnp.sum(jnp.where(same & (down < along), 1.0, 0.0), axis=0, keepdims=True)
+    slot_col = jnp.sum(jnp.where(same & (along < down), 1.0, 0.0), axis=1, keepdims=True)
+    owners = 2 * chips
+    spot_of = slot_row * owners + codes[2:3, :]
+    hot = jnp.where(lax.broadcasted_iota(I32, (cap * owners, blocks), 0).astype(F32) == spot_of, 1.0, 0.0).astype(BF16)
+    slots = folded(dot(hot, jnp.concatenate(split(mass_v[...]), axis=1)))
+    mark = slot_col * tags + flipped[:, 3:4]
+    marked = jnp.where(lax.broadcasted_iota(I32, (blocks, points), 1).astype(F32) == mark, 1.0, 0.0).astype(BF16)
+    owner_hot = jnp.where(lax.broadcasted_iota(I32, (owners, blocks), 0).astype(F32) == codes[2:3, :], 1.0, 0.0).astype(BF16)
+    marks = dot(owner_hot, marked)
+    for s in range(2):
+        for j in range(cap):
+            slot_own[s, :, j, :] = slots[j * owners + s * chips : j * owners + (s + 1) * chips]
+        slot_own[s, :, cap, :] = marks[s * chips : (s + 1) * chips]
+
     loads["table"].wait()
     for p in range(patterns):
         th, tl = split(table_v[p])
         spot = slice(p * points, (p + 1) * points)
         nn_w[spot, :points] = th
         nn_w[spot, points:] = tl
-        nt_w[spot, :points] = th
-        nt_w[spot, points:] = th
-        nt_lo[spot, :] = tl
-
-    def folded(pair):
-        return pair[:, :points] + pair[:, points:]
 
     def project(values):
         parts = []
@@ -230,33 +247,12 @@
         done.extend(copies)
         return copies
 
-    loads["mass"].wait()
     loads["prev"].wait()
     loads["base"].wait()
     force = project([base_v[c] - mass_v[...] * prev_v[c] for c in range(3)])
     for c in range(3):
         d_all[c] = folded(dot(scatter_hot[c], force[c]))
     pl.semaphore_wait(barrier, len(partners))
-    core0 = to_sibling(0)
-
-    owner_col = lax.broadcast_in_dim(flipped[:, 2:3], (blocks, blocks), (0, 1))
-    same = owner_col == codes[2:3, :]
-    down = lax.broadcasted_iota(I32, (blocks, blocks), 0)
-    along = lax.broadcasted_iota(I32, (blocks, blocks), 1)
-    slot_row = jnp.sum(jnp.where(same & (down < along), 1.0, 0.0), axis=0, keepdims=True)
-    slot_col = jnp.sum(jnp.where(same & (along < down), 1.0, 0.0), axis=1, keepdims=True)
-    owners = 2 * chips
-    spot_of = slot_row * owners + codes[2:3, :]
-    hot = jnp.where(lax.broadcasted_iota(I32, (cap * owners, blocks), 0).astype(F32) == spot_of, 1.0, 0.0).astype(BF16)
-    slots = folded(dot(hot, jnp.concatenate(split(mass_v[...]), axis=1)))
-    mark = slot_col * tags + flipped[:, 3:4]
-    marked = jnp.where(lax.broadcasted_iota(I32, (blocks, points), 1).astype(F32) == mark, 1.0, 0.0).astype(BF16)
-    owner_hot = jnp.where(lax.broadcasted_iota(I32, (owners, blocks), 0).astype(F32) == codes[2:3, :], 1.0, 0.0).astype(BF16)
-    marks = dot(owner_hot, marked)
-    for s in range(2):
-        for j in range(cap):
-            slot_own[s, :, j, :] = slots[j * owners + s * chips : j * owners + (s + 1) * chips]
-        slot_own[s, :, cap, :] = marks[s * chips : (s + 1) * chips]
     slot_copy = pltpu.make_async_remote_copy(
         src_ref=slot_own.at[1 - core],
         dst_ref=slot_out.at[core],
@@ -266,13 +262,10 @@
         device_id_type=MESH,
     )
     slot_copy.start()
+    core0 = to_sibling(0)
     slot_out[core] = slot_own[core]
     chip = (z * n + y) * n + x
     axis0 = stage0(0, core0)
-    load = project([base_v[c] for c in range(3)])
-    for c in range(3):
-        d_all[3 + c] = folded(dot(scatter_hot[c], load[c]))
-    core1 = to_sibling(1)
     slot_copy.wait_recv()
     done.append(slot_copy)
     slot_in[:, chip] = slot_out[:, chip]
@@ -286,6 +279,10 @@
             device_id=shifted(dx, dy, dz),
             device_id_type=MESH,
         ).start()
+    load = project([base_v[c] for c in range(3)])
+    for c in range(3):
+        d_all[3 + c] = folded(dot(scatter_hot[c], load[c]))
+    core1 = to_sibling(1)
 
     loads["stiff"].wait()
     loads["srow"].wait()
@@ -294,7 +291,6 @@
     for i in range(stiff_v.shape[0]):
         stiff_hi[i], stiff_lo[i] = split(stiff_v[i].T)
 
-    axis1 = stage0(1, core1)
 
     flat = sorted(((a, b) for a in range(n) for b in range(n) if a or b), key=far, reverse=True)
 
@@ -345,6 +341,7 @@
         return jnp.concatenate(ends, axis=1)
 
     stage1(0, axis0)
+    axis1 = stage0(1, core1)
 
     def stacked(value):
         vh, vl = split(value)
@@ -396,8 +393,9 @@
     for i in range(cols):
         inverse_hi[i], inverse_lo[i] = split(inverse_v[i].T)
     flipped = codes[...].T
-    lane = lax.broadcasted_iota(I32, (blocks, keys), 1).astype(F32)
-    gather_hot[...] = jnp.where(lane == flipped[:, 0:1], 1.0, 0.0).astype(BF16)
+    lane = lax.broadcasted_iota(I32, (blocks, half), 1).astype(F32)
+    for side in range(2):
+        gather_hot[side] = jnp.where(lane == flipped[:, 0:1] - side * half, 1.0, 0.0).astype(BF16)
 
     def correct(residual):
         lhs = stacked(residual)
@@ -409,6 +407,12 @@
             total = total + jnp.where(col_at == k, a[0:cols] + a[cols : 2 * cols] + b[0:cols], 0.0)
         return total
 
+    for p in range(patterns):
+        th, tl = split(table_v[p].T)
+        spot = slice(p * points, (p + 1) * points)
+        nt_w[:points, spot] = th
+        nt_w[points:, spot] = th
+        nt_lo[:, spot] = tl
     stage1(1, axis1)
     field1 = field0 + correct(plane_end(0) - coupled(0, cpl_copies0))
     cpl_copies1 = couple(field1, 1)
@@ -417,7 +421,7 @@
     for c in range(3):
         rows_s[c * cols : (c + 1) * cols, :] = field1[:, c * points : (c + 1) * points]
     uh, ul = split(rows_s[...])
-    spread = dot(jnp.concatenate([uh, ul], axis=1), nt_w[...], NT) + dot(uh, nt_lo[...], NT)
+    spread = dot(jnp.concatenate([uh, ul], axis=1), nt_w[...]) + dot(uh, nt_lo[...])
 
     arrived = all_of(slot_in.at[:, pl.ds(0, chips - 1)], slot_send, slot_recv)
     arrived.wait_recv()
@@ -444,43 +448,54 @@
         out_u[c] = field2[:, c * points : (c + 1) * points]
     home = pl.multiple_of(core * chips, 8)
     field[home + chip] = field2
-    for offsets in everywhere:
-        pltpu.make_async_remote_copy(
-            src_ref=field.at[home + chip],
-            dst_ref=field.at[home + chip],
-            send_sem=back_send,
-            recv_sem=back_recv,
-            device_id=shifted(*offsets),
+    planes = sorted(range(n), key=lambda d: -min(d, n - d))
+    for dz in planes:
+        for offsets in everywhere:
+            if offsets[2] == dz:
+                pltpu.make_async_remote_copy(
+                    src_ref=field.at[home + chip],
+                    dst_ref=field.at[home + chip],
+                    send_sem=back_send.at[dz],
+                    recv_sem=back_recv.at[dz],
+                    device_id=shifted(*offsets),
+                    device_id_type=MESH,
+                ).start()
+    homes = []
+    for dz in planes:
+        first_row = home + lax.rem(z - dz + n, n) * (n * n)
+        copy = all_of(field.at[pl.ds(first_row, n * n if dz else n * n - 1)], back_send.at[dz], back_recv.at[dz])
+        copy.wait_recv()
+        done.append(copy)
+        view = field.at[pl.ds(first_row, n * n)]
+        copy = pltpu.make_async_remote_copy(
+            src_ref=view,
+            dst_ref=view,
+            send_sem=home_send.at[dz],
+            recv_sem=home_recv.at[dz],
+            device_id=sibling,
             device_id_type=MESH,
-        ).start()
-    copy = all_of(field.at[pl.ds(home, chips - 1)], back_send, back_recv)
-    copy.wait_recv()
-    done.append(copy)
-    view = field.at[pl.ds(home, chips)]
-    copy = pltpu.make_async_remote_copy(
-        src_ref=view,
-        dst_ref=view,
-        send_sem=home_send,
-        recv_sem=home_recv,
-        device_id=sibling,
-        device_id_type=MESH,
-    )
-    copy.start()
-    copy.wait_recv()
-    done.append(copy)
-
+        )
+        copy.start()
+        homes.append(copy)
+        done.append(copy)
+
+    def gathered(side):
+        fh, fl = split(field[pl.ds(side * chips, chips)].reshape(half, width))
+        hot = gather_hot[side]
+        spots = [slice(c * points, (c + 1) * points) for c in range(3)]
+        return [dot(hot, jnp.concatenate([fh[:, spot], fl[:, spot]], axis=1)) for spot in spots]
+
+    near = gathered(core)
+    for copy in homes:
+        copy.wait_recv()
     flipped = codes[...].T
     pattern_col = flipped[:, 1:2]
-    fh, fl = split(field[...].reshape(keys, width))
-    rows = []
-    for c in range(3):
-        spot = slice(c * points, (c + 1) * points)
-        rows.append(dot(gather_hot[...], jnp.concatenate([fh[:, spot], fl[:, spot]], axis=1)).astype(BF16))
+    rows = [(u + v).astype(BF16) for u, v in zip(near, gathered(1 - core))]
     got = jnp.concatenate(rows, axis=0)
     acc = [jnp.zeros((blocks, points), F32) for _ in range(3)]
     for j in range(patterns // 2):
         spot = slice(2 * j * points, 2 * (j + 1) * points)
-        pair = dot(got, nt_w[spot, :], NT) + dot(got[:, :points], nt_lo[spot, :], NT)
+        pair = dot(got, nt_w[:, spot]) + dot(got[:, :points], nt_lo[:, spot])
         for c in range(3):
             mid = pair[c * blocks : (c + 1) * blocks]
             acc[c] = jnp.where(pattern_col == 2 * j, mid[:, :points], acc[c])
@@ -521,8 +536,8 @@
     out_u, out_i = pl.pallas_call(
         functools.partial(kernel, n),
         out_shape=(
-            jax.ShapeDtypeStruct((3, cols, points), F32),
-            jax.ShapeDtypeStruct((3, blocks, points), F32),
+            pltpu.VMEM((3, cols, points), F32),
+            pltpu.VMEM((3, blocks, points), F32),
         ),
         in_specs=[any_] * 12,
         out_specs=(vmem, vmem),
@@ -544,12 +559,12 @@
             V((cols, width, width), BF16),
             V((cols, width, width), BF16),
             V((patterns * points, 2 * points), BF16),
-            V((patterns * points, 2 * points), BF16),
-            V((patterns * points, points), BF16),
+            V((2 * points, patterns * points), BF16),
+            V((points, patterns * points), BF16),
             V((128, blocks), F32),
             V((patterns, blocks, points), BF16),
             V((3, keys, blocks), BF16),
-            V((blocks, keys), BF16),
+            V((2, blocks, half), BF16),
             V((6, keys, points), F32),
             V((6, half, points), F32),
             V((n - 1, 6, rows1, points), F32),
@@ -574,10 +589,10 @@
             dma,
             dma((2, n - 1)),
             dma((2, n - 1)),
-            dma,
-            dma,
-            dma,
-            dma,
+            dma((n,)),
+            dma((n,)),
+            dma((n,)),
+            dma((n,)),
         ],
         compiler_params=pltpu.CompilerParams(
             collective_id=0, has_side_effects=True, vmem_limit_bytes=62 * 1024 * 1024

time: 43.7 us -> 40.5 us (0.927)
  local copies, waits for them, and re-layouts: 3.05 us -> 1.34 us
  Pallas kernels: 39.8 us -> 38.4 us
    unnamed x2, local copies, waits for them, and re-layouts: 3.05 us -> 1.34 us
    pallas_call x1, Pallas kernels: 39.8 us -> 38.4 us  [on_device(): pl.pallas_call(functools.partial(kernel, n), out_shape=(pltpu.VMEM((3, co...]
where the time goes in v4:
time: 40.5 us; the launch traced here: 40.4 us
  Pallas kernels  38.4 us (95%)
  local copies, waits for them, and re-layouts  1.34 us (3%)
  between operations  0.64 us (2%)
    pallas_call x1, Pallas kernels, on_device(): pl.pallas_call(functools.partial(kernel, n), out_shape=(pltpu.VMEM((3, co...  38.4 us
    unnamed x2, local copies, waits for them, and re-layouts  1.34 us

profile of v4, /device:TPU:1, one launch (start us, length us, event | category | flops | bytes accessed | tf_op | source)
XLA Modules:
  0.0 40.4 jit_solution(15032708353245155733)
XLA Ops:
  0.6 38.4 %shard_map.131 = (f32[3,4,128]{2,1,0:T(4,128)S(1)}, f32[3,256,128]{2,1,0:T(8,128)S(1)}) custom-call(f32[3,256,128]{2,1,0:T(8,128)} %bitcast.10, f32[256,128]{1,0:T(8,128)} %mass_h.1, f32[3,256,128]{2,1,0:T(8,128)} %bitcast.11, s32[1,256]{1,0:T(1,128)} %bitcast.13, s32[1,256]{1,0:T(1,128)} %bitcast.14, s32[1,256]{1,0:T(1,128)} %bitcast.15, ...), custom_call_target="tpu_custom_call" | custom-call | tf_op jit(solution)/shard_map/pallas_call | solution.py:536
  39.1 0.6 %copy.16 = f32[4,3,128]{2,0,1:T(4,128)} copy(f32[4,3,128]{2,0,1:T(4,128)S(1)} %bitcast.9) | data formatting | bytes 12288
  39.7 0.7 %copy.17 = f32[256,3,128]{2,0,1:T(8,128)} copy(f32[256,3,128]{2,0,1:T(8,128)S(1)} %bitcast.8) | data formatting | bytes 786432

commit v5 on v4

--- a/solution.py
+++ b/solution.py
@@ -266,19 +266,6 @@
     slot_out[core] = slot_own[core]
     chip = (z * n + y) * n + x
     axis0 = stage0(0, core0)
-    slot_copy.wait_recv()
-    done.append(slot_copy)
-    slot_in[:, chip] = slot_out[:, chip]
-    for dx, dy, dz in everywhere:
-        to = (lax.rem(z + dz, n) * n + lax.rem(y + dy, n)) * n + lax.rem(x + dx, n)
-        pltpu.make_async_remote_copy(
-            src_ref=slot_out.at[:, to],
-            dst_ref=slot_in.at[:, chip],
-            send_sem=slot_send,
-            recv_sem=slot_recv,
-            device_id=shifted(dx, dy, dz),
-            device_id_type=MESH,
-        ).start()
     load = project([base_v[c] for c in range(3)])
     for c in range(3):
         d_all[3 + c] = folded(dot(scatter_hot[c], load[c]))
@@ -291,6 +278,8 @@
     for i in range(stiff_v.shape[0]):
         stiff_hi[i], stiff_lo[i] = split(stiff_v[i].T)
 
+
+    axis1 = stage0(1, core1)
 
     flat = sorted(((a, b) for a in range(n) for b in range(n) if a or b), key=far, reverse=True)
 
@@ -341,7 +330,6 @@
         return jnp.concatenate(ends, axis=1)
 
     stage1(0, axis0)
-    axis1 = stage0(1, core1)
 
     def stacked(value):
         vh, vl = split(value)
@@ -388,6 +376,20 @@
 
     field0 = jnp.concatenate([start_v[c] for c in range(3)], axis=1)
     cpl_copies0 = couple(field0, 0)
+
+    slot_copy.wait_recv()
+    done.append(slot_copy)
+    slot_in[:, chip] = slot_out[:, chip]
+    for dx, dy, dz in everywhere:
+        to = (lax.rem(z + dz, n) * n + lax.rem(y + dy, n)) * n + lax.rem(x + dx, n)
+        pltpu.make_async_remote_copy(
+            src_ref=slot_out.at[:, to],
+            dst_ref=slot_in.at[:, chip],
+            send_sem=slot_send,
+            recv_sem=slot_recv,
+            device_id=shifted(dx, dy, dz),
+            device_id_type=MESH,
+        ).start()
 
     loads["inverse"].wait()
     for i in range(cols):
@@ -505,6 +507,14 @@
 
     for copy in done:
         copy.wait_send()
+
+
+def deliver(u_ref, i_ref, out_u, out_i, sem):
+    copies = [pltpu.make_async_copy(src, dst, sem.at[k]) for k, (src, dst) in enumerate(((i_ref, out_i), (u_ref, out_u)))]
+    for copy in copies:
+        copy.start()
+    for copy in copies:
+        copy.wait()
 
 
 def on_device(
@@ -611,6 +621,17 @@
         block_inverse,
         jnp.transpose(previous_shell_displacement, (1, 0, 2)),
     )
+    out_u, out_i = pl.pallas_call(
+        deliver,
+        out_shape=(
+            jax.ShapeDtypeStruct((3, cols, points), F32),
+            jax.ShapeDtypeStruct((3, blocks, points), F32),
+        ),
+        in_specs=[vmem, vmem],
+        out_specs=(any_, any_),
+        scratch_shapes=[dma((2,))],
+        compiler_params=pltpu.CompilerParams(vmem_limit_bytes=4 * 1024 * 1024),
+    )(*(pltpu.with_memory_space_constraint(v, pltpu.VMEM) for v in (out_u, out_i)))
     return jnp.transpose(out_u, (1, 0, 2)), jnp.transpose(out_i, (1, 0, 2))
 
 

time: 40.5 us -> 39.2 us (0.968)
  local copies, waits for them, and re-layouts: 1.34 us -> 0 us
    unnamed x2 -> x0, local copies, waits for them, and re-layouts: 1.34 us -> none
    pallas_call x0 -> x1, Pallas kernels: none -> 0.77 us  [on_device(): pl.pallas_call(deliver, out_shape=(jax.ShapeDtypeStruct((3, cols, points)...]
    pallas_call x1, Pallas kernels: 38.4 us -> 37.7 us  [on_device(): pl.pallas_call(functools.partial(kernel, n), out_shape=(pltpu.VMEM((3, co...]
where the time goes in v5:
time: 39.2 us; the launch traced here: 39.1 us
  Pallas kernels  38.5 us (98%)
  between operations  0.64 us (2%)
    pallas_call x1, Pallas kernels, on_device(): pl.pallas_call(functools.partial(kernel, n), out_shape=(pltpu.VMEM((3, co...  37.7 us

profile of v5, /device:TPU:1, one launch (start us, length us, event | category | flops | bytes accessed | tf_op | source)
XLA Modules:
  0.0 39.1 jit_solution(13139009384539391909)
XLA Ops:
  0.6 37.7 %shard_map.131 = (f32[3,4,128]{2,1,0:T(4,128)S(1)}, f32[3,256,128]{2,1,0:T(8,128)S(1)}) custom-call(f32[3,256,128]{2,1,0:T(8,128)} %bitcast.8, f32[256,128]{1,0:T(8,128)} %mass_h.1, f32[3,256,128]{2,1,0:T(8,128)} %bitcast.9, s32[1,256]{1,0:T(1,128)} %bitcast.11, s32[1,256]{1,0:T(1,128)} %bitcast.12, s32[1,256]{1,0:T(1,128)} %bitcast.13, ...), custom_call_target="tpu_custom_call" | custom-call | tf_op jit(solution)/shard_map/pallas_call | solution.py:546
  38.3 0.8 %shard_map.132 = (f32[3,4,128]{2,1,0:T(4,128)}, f32[3,256,128]{2,1,0:T(8,128)}) custom-call(f32[3,4,128]{2,1,0:T(4,128)S(1)} %get-tuple-element.6.u_ref, f32[3,256,128]{2,1,0:T(8,128)S(1)} %get-tuple-element.7.i_ref), custom_call_target="tpu_custom_call" | custom-call | tf_op jit(solution)/shard_map/pallas_call | solution.py:624

commit v6 on v5

--- a/solution.py
+++ b/solution.py
@@ -59,6 +59,7 @@
     pmask,
     scatter_hot,
     gather_hot,
+    pattern_wide,
     d_all,
     c_all,
     r1_all,
@@ -75,6 +76,7 @@
     load_sem,
     core_send,
     core_recv,
+    ready,
     axis_send,
     axis_recv,
     plane_send,
@@ -129,7 +131,8 @@
         loads[name].start()
 
     barrier = pltpu.get_barrier_semaphore()
-    partners = [sibling] + [shifted(*o) for o in everywhere]
+    beside = [shifted(*[step if a == axis else 0 for a in range(3)]) for axis in range(3) for step in range(1, n)]
+    partners = [sibling] + beside
     for partner in partners:
         pl.semaphore_signal(barrier, inc=1, device_id=partner, device_id_type=MESH)
 
@@ -161,7 +164,81 @@
     for part in range(3):
         scatter_hot[part] = jnp.where(sub == code[part], 1.0, 0.0).astype(BF16)
 
+    loads["table"].wait()
+    for p in range(patterns):
+        th, tl = split(table_v[p])
+        spot = slice(p * points, (p + 1) * points)
+        nn_w[spot, :points] = th
+        nn_w[spot, points:] = tl
+
+    def project(values):
+        parts = []
+        for value in values:
+            parts.extend(split(value))
+        wide = jnp.concatenate(
+            [jnp.concatenate([v * pmask[p] for v in parts], axis=0) for p in range(patterns)], axis=1
+        )
+        got = dot(wide, nn_w[...])
+        ends = []
+        for i in range(3):
+            both = got[2 * i * blocks : (2 * i + 1) * blocks] + got[(2 * i + 1) * blocks : (2 * i + 2) * blocks]
+            ends.append(jnp.concatenate(split(folded(both)), axis=1))
+        return ends
+
+    other = pl.multiple_of((1 - core) * half, 8)
+    mine = pl.multiple_of(core * half, 8)
+
+    def to_sibling(t, count):
+        copy = pltpu.make_async_remote_copy(
+            src_ref=d_all.at[t : t + count, pl.ds(other, half), :],
+            dst_ref=c_all.at[t : t + count],
+            send_sem=core_send.at[t],
+            recv_sem=core_recv.at[t],
+            device_id=sibling,
+            device_id_type=MESH,
+        )
+        copy.start()
+        return copy
+
+    done = []
+
+    def stage0(group, arriving):
+        copies = []
+        for part in range(3):
+            if part < len(arriving):
+                arriving[part].wait_recv()
+                done.append(arriving[part])
+            t = 3 * group + part
+            c_all[t] = c_all[t] + d_all[t, pl.ds(mine, half), :]
+            axis = axes[part][0]
+            for step in range(1, n):
+                to = lax.rem(place[axis] + step, n)
+                slot = part * (n - 1) + step - 1
+                copies.append(
+                    pltpu.make_async_remote_copy(
+                        src_ref=c_all.at[t, pl.ds(pl.multiple_of(to * rows1, 8), rows1), :],
+                        dst_ref=r1_all.at[step - 1, t],
+                        send_sem=axis_send.at[group, slot],
+                        recv_sem=axis_recv.at[group, slot],
+                        device_id=shifted(*[step if a == axis else 0 for a in range(3)]),
+                        device_id_type=MESH,
+                    )
+                )
+                copies[-1].start()
+        done.extend(copies)
+        return copies
+
     loads["mass"].wait()
+    loads["prev"].wait()
+    loads["base"].wait()
+    force = project([base_v[c] - mass_v[...] * prev_v[c] for c in range(3)])
+    pl.semaphore_wait(barrier, len(partners))
+    for partner in beside:
+        pl.semaphore_signal(ready.at[0], inc=1, device_id=partner, device_id_type=MESH)
+    core0 = []
+    for c in range(3):
+        d_all[c] = folded(dot(scatter_hot[c], force[c]))
+        core0.append(to_sibling(c, 1))
     owner_col = lax.broadcast_in_dim(flipped[:, 2:3], (blocks, blocks), (0, 1))
     same = owner_col == codes[2:3, :]
     down = lax.broadcasted_iota(I32, (blocks, blocks), 0)
@@ -180,96 +257,42 @@
         for j in range(cap):
             slot_own[s, :, j, :] = slots[j * owners + s * chips : j * owners + (s + 1) * chips]
         slot_own[s, :, cap, :] = marks[s * chips : (s + 1) * chips]
-
-    loads["table"].wait()
-    for p in range(patterns):
-        th, tl = split(table_v[p])
-        spot = slice(p * points, (p + 1) * points)
-        nn_w[spot, :points] = th
-        nn_w[spot, points:] = tl
-
-    def project(values):
-        parts = []
-        for value in values:
-            parts.extend(split(value))
-        wide = jnp.concatenate(
-            [jnp.concatenate([v * pmask[p] for v in parts], axis=0) for p in range(patterns)], axis=1
-        )
-        got = dot(wide, nn_w[...])
-        ends = []
-        for i in range(3):
-            both = got[2 * i * blocks : (2 * i + 1) * blocks] + got[(2 * i + 1) * blocks : (2 * i + 2) * blocks]
-            ends.append(jnp.concatenate(split(folded(both)), axis=1))
-        return ends
-
-    other = pl.multiple_of((1 - core) * half, 8)
-    mine = pl.multiple_of(core * half, 8)
-
-    def to_sibling(group):
-        low_t, high_t = 3 * group, 3 * group + 3
-        copy = pltpu.make_async_remote_copy(
-            src_ref=d_all.at[low_t:high_t, pl.ds(other, half), :],
-            dst_ref=c_all.at[low_t:high_t],
-            send_sem=core_send.at[group],
-            recv_sem=core_recv.at[group],
-            device_id=sibling,
-            device_id_type=MESH,
-        )
-        copy.start()
-        return copy
-
-    done = []
-
-    def stage0(group, copy):
-        copy.wait_recv()
-        done.append(copy)
-        for t in range(3 * group, 3 * group + 3):
-            c_all[t] = c_all[t] + d_all[t, pl.ds(mine, half), :]
-        copies = []
-        for step in range(1, n):
-            for part in range(3):
-                axis = axes[part][0]
-                t = 3 * group + part
-                to = lax.rem(place[axis] + step, n)
-                slot = part * (n - 1) + step - 1
-                target = shifted(*[step if a == axis else 0 for a in range(3)])
-                copies.append(
-                    pltpu.make_async_remote_copy(
-                        src_ref=c_all.at[t, pl.ds(pl.multiple_of(to * rows1, 8), rows1), :],
-                        dst_ref=r1_all.at[step - 1, t],
-                        send_sem=axis_send.at[group, slot],
-                        recv_sem=axis_recv.at[group, slot],
-                        device_id=target,
-                        device_id_type=MESH,
-                    )
-                )
-                copies[-1].start()
-        done.extend(copies)
-        return copies
-
-    loads["prev"].wait()
-    loads["base"].wait()
-    force = project([base_v[c] - mass_v[...] * prev_v[c] for c in range(3)])
-    for c in range(3):
-        d_all[c] = folded(dot(scatter_hot[c], force[c]))
-    pl.semaphore_wait(barrier, len(partners))
     slot_copy = pltpu.make_async_remote_copy(
         src_ref=slot_own.at[1 - core],
         dst_ref=slot_out.at[core],
-        send_sem=core_send.at[2],
-        recv_sem=core_recv.at[2],
+        send_sem=core_send.at[4],
+        recv_sem=core_recv.at[4],
         device_id=sibling,
         device_id_type=MESH,
     )
     slot_copy.start()
-    core0 = to_sibling(0)
     slot_out[core] = slot_own[core]
     chip = (z * n + y) * n + x
     axis0 = stage0(0, core0)
+    pl.semaphore_wait(ready.at[0], len(beside))
+    for partner in beside:
+        pl.semaphore_signal(ready.at[1], inc=1, device_id=partner, device_id_type=MESH)
     load = project([base_v[c] for c in range(3)])
     for c in range(3):
         d_all[3 + c] = folded(dot(scatter_hot[c], load[c]))
-    core1 = to_sibling(1)
+    core1 = to_sibling(3, 3)
+    pl.semaphore_wait(ready.at[1], len(beside))
+    slot_copy.wait_recv()
+    done.append(slot_copy)
+    slot_in[:, chip] = slot_out[:, chip]
+
+    def send_slots(some):
+        for dx, dy, dz in some:
+            to = (lax.rem(z + dz, n) * n + lax.rem(y + dy, n)) * n + lax.rem(x + dx, n)
+            pltpu.make_async_remote_copy(
+                src_ref=slot_out.at[:, to],
+                dst_ref=slot_in.at[:, chip],
+                send_sem=slot_send,
+                recv_sem=slot_recv,
+                device_id=shifted(dx, dy, dz),
+                device_id_type=MESH,
+            ).start()
+
 
     loads["stiff"].wait()
     loads["srow"].wait()
@@ -279,7 +302,7 @@
         stiff_hi[i], stiff_lo[i] = split(stiff_v[i].T)
 
 
-    axis1 = stage0(1, core1)
+    axis1 = stage0(1, [core1])
 
     flat = sorted(((a, b) for a in range(n) for b in range(n) if a or b), key=far, reverse=True)
 
@@ -377,25 +400,14 @@
     field0 = jnp.concatenate([start_v[c] for c in range(3)], axis=1)
     cpl_copies0 = couple(field0, 0)
 
-    slot_copy.wait_recv()
-    done.append(slot_copy)
-    slot_in[:, chip] = slot_out[:, chip]
-    for dx, dy, dz in everywhere:
-        to = (lax.rem(z + dz, n) * n + lax.rem(y + dy, n)) * n + lax.rem(x + dx, n)
-        pltpu.make_async_remote_copy(
-            src_ref=slot_out.at[:, to],
-            dst_ref=slot_in.at[:, chip],
-            send_sem=slot_send,
-            recv_sem=slot_recv,
-            device_id=shifted(dx, dy, dz),
-            device_id_type=MESH,
-        ).start()
+    send_slots(everywhere)
 
     loads["inverse"].wait()
     for i in range(cols):
         inverse_hi[i], inverse_lo[i] = split(inverse_v[i].T)
     flipped = codes[...].T
     lane = lax.broadcasted_iota(I32, (blocks, half), 1).astype(F32)
+    pattern_wide[...] = jnp.broadcast_to(flipped[:, 1:2], (blocks, points))
     for side in range(2):
         gather_hot[side] = jnp.where(lane == flipped[:, 0:1] - side * half, 1.0, 0.0).astype(BF16)
 
@@ -408,6 +420,7 @@
             b = dot(lhs, inverse_lo[k])
             total = total + jnp.where(col_at == k, a[0:cols] + a[cols : 2 * cols] + b[0:cols], 0.0)
         return total
+
 
     for p in range(patterns):
         th, tl = split(table_v[p].T)
@@ -490,18 +503,17 @@
     near = gathered(core)
     for copy in homes:
         copy.wait_recv()
-    flipped = codes[...].T
-    pattern_col = flipped[:, 1:2]
     rows = [(u + v).astype(BF16) for u, v in zip(near, gathered(1 - core))]
     got = jnp.concatenate(rows, axis=0)
+    pattern_at = pattern_wide[...]
     acc = [jnp.zeros((blocks, points), F32) for _ in range(3)]
     for j in range(patterns // 2):
         spot = slice(2 * j * points, 2 * (j + 1) * points)
         pair = dot(got, nt_w[:, spot]) + dot(got[:, :points], nt_lo[:, spot])
         for c in range(3):
             mid = pair[c * blocks : (c + 1) * blocks]
-            acc[c] = jnp.where(pattern_col == 2 * j, mid[:, :points], acc[c])
-            acc[c] = jnp.where(pattern_col == 2 * j + 1, mid[:, points:], acc[c])
+            acc[c] = jnp.where(pattern_at == 2 * j, mid[:, :points], acc[c])
+            acc[c] = jnp.where(pattern_at == 2 * j + 1, mid[:, points:], acc[c])
     for c in range(3):
         out_i[c] = acc[c]
 
@@ -575,6 +587,7 @@
             V((patterns, blocks, points), BF16),
             V((3, keys, blocks), BF16),
             V((2, blocks, half), BF16),
+            V((blocks, points), F32),
             V((6, keys, points), F32),
             V((6, half, points), F32),
             V((n - 1, 6, rows1, points), F32),
@@ -589,8 +602,9 @@
             V((16, patterns * points), F32),
             V((2 * chips, cols, width), F32),
             dma((12,)),
-            dma((3,)),
-            dma((3,)),
+            dma((5,)),
+            dma((5,)),
+            pltpu.SemaphoreType.REGULAR((2,)),
             dma((2, 3 * (n - 1))),
             dma((2, 3 * (n - 1))),
             dma((2,)),

time: 39.2 us -> 37.9 us (0.967)
  Pallas kernels: 38.5 us -> 37.2 us
    pallas_call x1, Pallas kernels: 37.7 us -> 36.4 us  [on_device(): pl.pallas_call(functools.partial(kernel, n), out_shape=(pltpu.VMEM((3, co...]
where the time goes in v6:
time: 37.9 us; the launch traced here: 37.8 us
  Pallas kernels  37.2 us (98%)
  between operations  0.64 us (2%)
    pallas_call x1, Pallas kernels, on_device(): pl.pallas_call(functools.partial(kernel, n), out_shape=(pltpu.VMEM((3, co...  36.4 us
    pallas_call x1, Pallas kernels, on_device(): pl.pallas_call(deliver, out_shape=(jax.ShapeDtypeStruct((3, cols, points)...  0.77 us

profile of v6, /device:TPU:1, one launch (start us, length us, event | category | flops | bytes accessed | tf_op | source)
XLA Modules:
  0.0 37.8 jit_solution(14838016545278611687)
XLA Ops:
  0.6 36.4 %shard_map.131 = (f32[3,4,128]{2,1,0:T(4,128)S(1)}, f32[3,256,128]{2,1,0:T(8,128)S(1)}) custom-call(f32[3,256,128]{2,1,0:T(8,128)} %bitcast.8, f32[256,128]{1,0:T(8,128)} %mass_h.1, f32[3,256,128]{2,1,0:T(8,128)} %bitcast.9, s32[1,256]{1,0:T(1,128)} %bitcast.11, s32[1,256]{1,0:T(1,128)} %bitcast.12, s32[1,256]{1,0:T(1,128)} %bitcast.13, ...), custom_call_target="tpu_custom_call" | custom-call | tf_op jit(solution)/shard_map/pallas_call | solution.py:558
  37.0 0.8 %shard_map.132 = (f32[3,4,128]{2,1,0:T(4,128)}, f32[3,256,128]{2,1,0:T(8,128)}) custom-call(f32[3,4,128]{2,1,0:T(4,128)S(1)} %get-tuple-element.6.u_ref, f32[3,256,128]{2,1,0:T(8,128)S(1)} %get-tuple-element.7.i_ref), custom_call_target="tpu_custom_call" | custom-call | tf_op jit(solution)/shard_map/pallas_call | solution.py:638

commit v7 on v6

--- a/solution.py
+++ b/solution.py
@@ -73,6 +73,7 @@
     rows_s,
     wide_s,
     field,
+    own_field,
     load_sem,
     core_send,
     core_recv,
@@ -111,6 +112,10 @@
     def shifted(dx, dy, dz):
         to_x, to_y, to_z = lax.rem(x + dx, n), lax.rem(y + dy, n), lax.rem(z + dz, n)
         return ((to_z * n + to_y) * 2 + core, to_x)
+
+    def crossed(dx, dy, dz):
+        to_x, to_y, to_z = lax.rem(x + dx, n), lax.rem(y + dy, n), lax.rem(z + dz, n)
+        return ((to_z * n + to_y) * 2 + 1 - core, to_x)
 
     def far(offsets):
         return sum(min(v, n - v) for v in offsets)
@@ -461,24 +466,25 @@
 
     for c in range(3):
         out_u[c] = field2[:, c * points : (c + 1) * points]
-    home = pl.multiple_of(core * chips, 8)
-    field[home + chip] = field2
+    home = pl.multiple_of((1 - core) * chips, 8)
+    away = core * chips + chip
+    own_field[...] = field2
     planes = sorted(range(n), key=lambda d: -min(d, n - d))
     for dz in planes:
-        for offsets in everywhere:
+        for offsets in everywhere + [(0, 0, 0)]:
             if offsets[2] == dz:
                 pltpu.make_async_remote_copy(
-                    src_ref=field.at[home + chip],
-                    dst_ref=field.at[home + chip],
+                    src_ref=own_field,
+                    dst_ref=field.at[away],
                     send_sem=back_send.at[dz],
                     recv_sem=back_recv.at[dz],
-                    device_id=shifted(*offsets),
+                    device_id=crossed(*offsets),
                     device_id_type=MESH,
                 ).start()
     homes = []
     for dz in planes:
         first_row = home + lax.rem(z - dz + n, n) * (n * n)
-        copy = all_of(field.at[pl.ds(first_row, n * n if dz else n * n - 1)], back_send.at[dz], back_recv.at[dz])
+        copy = all_of(field.at[pl.ds(first_row, n * n)], back_send.at[dz], back_recv.at[dz])
         copy.wait_recv()
         done.append(copy)
         view = field.at[pl.ds(first_row, n * n)]
@@ -500,10 +506,10 @@
         spots = [slice(c * points, (c + 1) * points) for c in range(3)]
         return [dot(hot, jnp.concatenate([fh[:, spot], fl[:, spot]], axis=1)) for spot in spots]
 
-    near = gathered(core)
+    near = gathered(1 - core)
     for copy in homes:
         copy.wait_recv()
-    rows = [(u + v).astype(BF16) for u, v in zip(near, gathered(1 - core))]
+    rows = [(u + v).astype(BF16) for u, v in zip(near, gathered(core))]
     got = jnp.concatenate(rows, axis=0)
     pattern_at = pattern_wide[...]
     acc = [jnp.zeros((blocks, points), F32) for _ in range(3)]
@@ -601,6 +607,7 @@
             V((16, points), F32),
             V((16, patterns * points), F32),
             V((2 * chips, cols, width), F32),
+            V((cols, width), F32),
             dma((12,)),
             dma((5,)),
             dma((5,)),

time: 37.9 us -> 36.6 us (0.966)
  Pallas kernels: 37.2 us -> 35.8 us
    pallas_call x1, Pallas kernels: 36.4 us -> 35.1 us  [on_device(): pl.pallas_call(functools.partial(kernel, n), out_shape=(pltpu.VMEM((3, co...]
where the time goes in v7:
time: 36.6 us; the launch traced here: 36.5 us
  Pallas kernels  35.8 us (98%)
  between operations  0.64 us (2%)
    pallas_call x1, Pallas kernels, on_device(): pl.pallas_call(functools.partial(kernel, n), out_shape=(pltpu.VMEM((3, co...  35.1 us
    pallas_call x1, Pallas kernels, on_device(): pl.pallas_call(deliver, out_shape=(jax.ShapeDtypeStruct((3, cols, points)...  0.77 us

profile of v7, /device:TPU:1, one launch (start us, length us, event | category | flops | bytes accessed | tf_op | source)
XLA Modules:
  0.0 36.5 jit_solution(2071782395766820738)
XLA Ops:
  0.6 35.1 %shard_map.131 = (f32[3,4,128]{2,1,0:T(4,128)S(1)}, f32[3,256,128]{2,1,0:T(8,128)S(1)}) custom-call(f32[3,256,128]{2,1,0:T(8,128)} %bitcast.8, f32[256,128]{1,0:T(8,128)} %mass_h.1, f32[3,256,128]{2,1,0:T(8,128)} %bitcast.9, s32[1,256]{1,0:T(1,128)} %bitcast.11, s32[1,256]{1,0:T(1,128)} %bitcast.12, s32[1,256]{1,0:T(1,128)} %bitcast.13, ...), custom_call_target="tpu_custom_call" | custom-call | tf_op jit(solution)/shard_map/pallas_call | solution.py:564
  35.7 0.8 %shard_map.132 = (f32[3,4,128]{2,1,0:T(4,128)}, f32[3,256,128]{2,1,0:T(8,128)}) custom-call(f32[3,4,128]{2,1,0:T(4,128)S(1)} %get-tuple-element.6.u_ref, f32[3,256,128]{2,1,0:T(8,128)S(1)} %get-tuple-element.7.i_ref), custom_call_target="tpu_custom_call" | custom-call | tf_op jit(solution)/shard_map/pallas_call | solution.py:645

commit v8 on v7

--- a/solution.py
+++ b/solution.py
@@ -54,7 +54,6 @@
     inverse_lo,
     nn_w,
     nt_w,
-    nt_lo,
     codes,
     pmask,
     scatter_hot,
@@ -431,8 +430,8 @@
         th, tl = split(table_v[p].T)
         spot = slice(p * points, (p + 1) * points)
         nt_w[:points, spot] = th
-        nt_w[points:, spot] = th
-        nt_lo[:, spot] = tl
+        nt_w[points : 2 * points, spot] = th
+        nt_w[2 * points :, spot] = tl
     stage1(1, axis1)
     field1 = field0 + correct(plane_end(0) - coupled(0, cpl_copies0))
     cpl_copies1 = couple(field1, 1)
@@ -441,7 +440,7 @@
     for c in range(3):
         rows_s[c * cols : (c + 1) * cols, :] = field1[:, c * points : (c + 1) * points]
     uh, ul = split(rows_s[...])
-    spread = dot(jnp.concatenate([uh, ul], axis=1), nt_w[...]) + dot(uh, nt_lo[...])
+    spread = dot(jnp.concatenate([uh, ul, uh], axis=1), nt_w[...])
 
     arrived = all_of(slot_in.at[:, pl.ds(0, chips - 1)], slot_send, slot_recv)
     arrived.wait_recv()
@@ -511,11 +510,12 @@
         copy.wait_recv()
     rows = [(u + v).astype(BF16) for u, v in zip(near, gathered(core))]
     got = jnp.concatenate(rows, axis=0)
+    got = jnp.concatenate([got, got[:, :points]], axis=1)
     pattern_at = pattern_wide[...]
     acc = [jnp.zeros((blocks, points), F32) for _ in range(3)]
     for j in range(patterns // 2):
         spot = slice(2 * j * points, 2 * (j + 1) * points)
-        pair = dot(got, nt_w[:, spot]) + dot(got[:, :points], nt_lo[:, spot])
+        pair = dot(got, nt_w[:, spot])
         for c in range(3):
             mid = pair[c * blocks : (c + 1) * blocks]
             acc[c] = jnp.where(pattern_at == 2 * j, mid[:, :points], acc[c])
@@ -528,7 +528,8 @@
 
 
 def deliver(u_ref, i_ref, out_u, out_i, sem):
-    copies = [pltpu.make_async_copy(src, dst, sem.at[k]) for k, (src, dst) in enumerate(((i_ref, out_i), (u_ref, out_u)))]
+    pairs = [(u_ref, out_u)] + [(i_ref.at[c], out_i.at[c]) for c in range(3)]
+    copies = [pltpu.make_async_copy(src, dst, sem.at[k]) for k, (src, dst) in enumerate(pairs)]
     for copy in copies:
         copy.start()
     for copy in copies:
@@ -587,8 +588,7 @@
             V((cols, width, width), BF16),
             V((cols, width, width), BF16),
             V((patterns * points, 2 * points), BF16),
-            V((2 * points, patterns * points), BF16),
-            V((points, patterns * points), BF16),
+            V((3 * points, patterns * points), BF16),
             V((128, blocks), F32),
             V((patterns, blocks, points), BF16),
             V((3, keys, blocks), BF16),
@@ -650,7 +650,7 @@
         ),
         in_specs=[vmem, vmem],
         out_specs=(any_, any_),
-        scratch_shapes=[dma((2,))],
+        scratch_shapes=[dma((4,))],
         compiler_params=pltpu.CompilerParams(vmem_limit_bytes=4 * 1024 * 1024),
     )(*(pltpu.with_memory_space_constraint(v, pltpu.VMEM) for v in (out_u, out_i)))
     return jnp.transpose(out_u, (1, 0, 2)), jnp.transpose(out_i, (1, 0, 2))

time: 36.6 us -> 36.6 us (level)
  no operation moved by 1% of the time
where the time goes in v8:
time: 36.6 us; the launch traced here: 36.5 us
  Pallas kernels  35.8 us (98%)
  between operations  0.64 us (2%)
    pallas_call x1, Pallas kernels, on_device(): pl.pallas_call(functools.partial(kernel, n), out_shape=(pltpu.VMEM((3, co...  35.1 us
    pallas_call x1, Pallas kernels, on_device(): pl.pallas_call(deliver, out_shape=(jax.ShapeDtypeStruct((3, cols, points)...  0.78 us

profile of v8, /device:TPU:1, one launch (start us, length us, event | category | flops | bytes accessed | tf_op | source)
XLA Modules:
  0.0 36.5 jit_solution(8656881754967969943)
XLA Ops:
  0.6 35.1 %shard_map.131 = (f32[3,4,128]{2,1,0:T(4,128)S(1)}, f32[3,256,128]{2,1,0:T(8,128)S(1)}) custom-call(f32[3,256,128]{2,1,0:T(8,128)} %bitcast.8, f32[256,128]{1,0:T(8,128)} %mass_h.1, f32[3,256,128]{2,1,0:T(8,128)} %bitcast.9, s32[1,256]{1,0:T(1,128)} %bitcast.11, s32[1,256]{1,0:T(1,128)} %bitcast.12, s32[1,256]{1,0:T(1,128)} %bitcast.13, ...), custom_call_target="tpu_custom_call" | custom-call | tf_op jit(solution)/shard_map/pallas_call | solution.py:565
  35.7 0.8 %shard_map.132 = (f32[3,4,128]{2,1,0:T(4,128)}, f32[3,256,128]{2,1,0:T(8,128)}) custom-call(f32[3,4,128]{2,1,0:T(4,128)S(1)} %get-tuple-element.6.u_ref, f32[3,256,128]{2,1,0:T(8,128)S(1)} %get-tuple-element.7.i_ref), custom_call_target="tpu_custom_call" | custom-call | tf_op jit(solution)/shard_map/pallas_call | solution.py:645
